TPU v7x, 32 devices: a whole 2x2x4 slice. The times are simulated.
32 devices in a mesh: seq: 8 (over z, x), ch: 4 (over y, core).
Axes of the slice: x: 2, y: 2, z: 4, core: 2. Of those that a mesh axis runs over, the one named last changes fastest.
Arguments:
- out_grad: float32 [128, 32768], P('ch', 'seq'), may hold values from -6 to 6
- gated_input: float32 [128, 32768], P('ch', 'seq'), may hold values from -6 to 6
- features: float32 [64, 32768], P(None, 'seq'), may hold values from -1 to 1
- filter_weight: float32 [64, 128], replicated, may hold values from -0.0078125 to 0.0078125
- rates: float32 [128], replicated, may hold values from 3 to 15
- skip_bias: float32 [128], replicated, may hold values from -3 to 3
Outputs:
- in_grad: float32 [128, 32768], P('ch', 'seq')
- feat_grad: float32 [64, 32768], P(None, ('seq', 'ch'))
All inputs are finite; a program needn't handle non-finite values.
Results may differ from a plain program's by a relative error of at most 0.0003.
Values sent between devices are 32-bit elements; how exact they have to be, the bound alone decides.
A program may use at most 128 MiB of HBM per device.

v0:
```python
import functools
import math

import jax
import jax.numpy as jnp
import numpy as np
from jax import lax
from jax.experimental import pallas as pl
from jax.experimental.pallas import tpu as pltpu
from jax.sharding import PartitionSpec as P

shift_term = 0.05
highest = lax.Precision.HIGHEST


def matmul_high(operand, matrix):
    return jnp.dot(operand, matrix, precision=highest, preferred_element_type=jnp.float32)


def angle_table(first_ids, second_ids, period):
    product = first_ids[:, None] * second_ids[None, :] % period
    angles = product.astype(jnp.float32) * (2.0 * math.pi / period)
    return (jnp.cos(angles), jnp.sin(angles))


def contract(real_part, imag_part, cos_table, sin_table, einsum_form):

    def multiply_by(operand, matrix):
        return jnp.einsum(
            einsum_form, operand, matrix, precision=highest, preferred_element_type=jnp.float32
        )

    return (
        multiply_by(real_part, cos_table) - multiply_by(imag_part, sin_table),
        multiply_by(real_part, sin_table) + multiply_by(imag_part, cos_table),
    )


def group_width(channels, block_len):
    return math.gcd(channels, max(1, 128 // block_len)) * block_len


def group_table(width, block_len, sign_term):
    ids = jnp.arange(width, dtype=jnp.int32)
    same = ids[:, None] // block_len == ids[None, :] // block_len
    inner = ids % block_len
    product = inner[:, None] * inner[None, :] % block_len
    angles = product.astype(jnp.float32) * (2.0 * math.pi / block_len)
    return (
        jnp.where(same, jnp.cos(angles), 0.0).astype(jnp.float32),
        jnp.where(same, sign_term * jnp.sin(angles), 0.0).astype(jnp.float32),
    )


def local_transform(real_part, imag_part, block_len, inverse):
    rows, seq_count, width_all = real_part.shape
    channels = width_all // block_len
    local_len = seq_count * block_len
    width = group_width(channels, block_len)
    sign_term = 1.0 if inverse else -1.0
    seq_ids = jnp.arange(seq_count, dtype=jnp.int32)
    block_ids = jnp.arange(block_len, dtype=jnp.int32)
    cos_seq, sin_seq = angle_table(seq_ids, seq_ids, seq_count)
    sin_seq = sign_term * sin_seq
    cos_twist, sin_twist = angle_table(seq_ids, block_ids, local_len)
    cos_twist = jnp.tile(cos_twist, (1, channels))
    sin_twist = sign_term * jnp.tile(sin_twist, (1, channels))
    cos_group, sin_group = group_table(width, block_len, sign_term)
    grouped = (rows, seq_count, width_all // width, width)
    flat = (rows, seq_count, width_all)

    def twist(re_part, im_part):
        return (
            re_part * cos_twist - im_part * sin_twist,
            re_part * sin_twist + im_part * cos_twist,
        )

    def across_groups(re_part, im_part):
        re_part, im_part = contract(
            re_part.reshape(grouped),
            im_part.reshape(grouped),
            cos_group,
            sin_group,
            "rkgm,mq->rkgq",
        )
        return (re_part.reshape(flat), im_part.reshape(flat))

    if inverse:
        real_part, imag_part = across_groups(real_part, imag_part)
        real_part, imag_part = twist(real_part, imag_part)
        real_part, imag_part = contract(real_part, imag_part, cos_seq, sin_seq, "rsx,sk->rkx")
    else:
        real_part, imag_part = contract(real_part, imag_part, cos_seq, sin_seq, "rsx,sk->rkx")
        real_part, imag_part = twist(real_part, imag_part)
        real_part, imag_part = across_groups(real_part, imag_part)
    return (real_part, imag_part)


def first_section(row_block, cos_fwd, sin_fwd, twid_cos, twid_sin):
    real_part = matmul_high(cos_fwd, row_block)
    imag_part = -matmul_high(sin_fwd, row_block)
    real_out = real_part * twid_cos + imag_part * twid_sin
    imag_out = imag_part * twid_cos - real_part * twid_sin
    return (real_out[:, None, :], imag_out[:, None, :])


def rotate_back(real_part, imag_part, twid_cos, twid_sin):
    return (
        real_part * twid_cos - imag_part * twid_sin,
        real_part * twid_sin + imag_part * twid_cos,
    )


def forward_products(
    block_len, grad_real, grad_imag, input_real, input_imag, filter_real, filter_imag
):
    grad_real, grad_imag = local_transform(grad_real, grad_imag, block_len, False)
    input_real, input_imag = local_transform(input_real, input_imag, block_len, False)
    filter_real, filter_imag = local_transform(filter_real, filter_imag, block_len, False)
    corr_real = filter_real * grad_real + filter_imag * grad_imag
    corr_imag = filter_real * grad_imag - filter_imag * grad_real
    lag_real = input_real * grad_real + input_imag * grad_imag
    lag_imag = input_real * grad_imag - input_imag * grad_real
    return (corr_real, corr_imag, lag_real, lag_imag)


def products_inverted(block_len, operands):
    corr_real, corr_imag, lag_real, lag_imag = forward_products(block_len, *operands)
    corr_real, corr_imag = local_transform(corr_real, corr_imag, block_len, True)
    lag_real, lag_imag = local_transform(lag_real, lag_imag, block_len, True)
    return (corr_real, corr_imag, lag_real, lag_imag)


def paired_rows(block_len, operands):
    seq_count = operands[0].shape[1]
    channels = operands[0].shape[2] // block_len
    local_len = seq_count * block_len
    positions = (
        jnp.arange(seq_count, dtype=jnp.int32)[:, None] * block_len
        + jnp.arange(block_len, dtype=jnp.int32)[None, :]
    )
    angles = positions.astype(jnp.float32) * (math.pi / local_len)
    half_cos = jnp.tile(jnp.cos(angles), (1, channels))
    half_sin = jnp.tile(jnp.sin(angles), (1, channels))
    stacked = []
    for index in range(3):
        low_row = operands[2 * index]
        high_row = operands[2 * index + 1]
        stacked.append(jnp.concatenate([low_row, high_row * half_cos], axis=0))
        stacked.append(jnp.concatenate([jnp.zeros_like(low_row), -high_row * half_sin], axis=0))
    corr_real, corr_imag, lag_real, lag_imag = products_inverted(block_len, tuple(stacked))
    return (
        corr_real[0:1],
        corr_real[1:2] * half_cos - corr_imag[1:2] * half_sin,
        lag_real[0:1],
        lag_real[1:2] * half_cos - lag_imag[1:2] * half_sin,
    )


def local(out_grad, gated_input, features, filter_weight, rates, skip_bias):
    channels, local_len = out_grad.shape
    seq_count = lax.axis_size("seq")
    block_len = local_len // seq_count
    width_all = channels * block_len
    freq_count = 2 * seq_count
    full_len = local_len * seq_count
    padded_len = 2 * full_len
    seq_place = lax.axis_index("seq")
    first_chan = lax.axis_index("ch") * channels
    local_rates = lax.dynamic_slice_in_dim(rates, first_chan, channels)
    local_bias = lax.dynamic_slice_in_dim(skip_bias, first_chan, channels)
    local_weight = lax.dynamic_slice_in_dim(filter_weight, first_chan, channels, 1)
    position = seq_place * local_len + jnp.arange(local_len, dtype=jnp.int32)
    window = (
        jnp.exp(-local_rates[:, None] * (position.astype(jnp.float32) / full_len)[None, :])
        + shift_term
    )
    filter_vals = matmul_high(local_weight.T, features) * window

    def to_rows(values):
        return (
            values.reshape(channels, seq_count, block_len)
            .transpose(1, 0, 2)
            .reshape(seq_count, width_all)
        )

    received = (
        lax.all_to_all(to_rows(out_grad), "seq", split_axis=0, concat_axis=0, tiled=True),
        lax.all_to_all(to_rows(gated_input), "seq", split_axis=0, concat_axis=0, tiled=True),
        lax.all_to_all(to_rows(filter_vals), "seq", split_axis=0, concat_axis=0, tiled=True),
    )

    def inverted(operands):
        return products_inverted(block_len, operands)

    def paired(operands):
        return paired_rows(block_len, operands)

    freq_ids = jnp.arange(freq_count, dtype=jnp.int32)
    dev_ids = jnp.arange(seq_count, dtype=jnp.int32)
    local_m = seq_place * block_len + jnp.arange(block_len, dtype=jnp.int32)
    twid_cos, twid_sin = angle_table(freq_ids, local_m, padded_len)
    twid_cos = jnp.tile(twid_cos, (1, channels))
    twid_sin = jnp.tile(twid_sin, (1, channels))
    scale_term = 1.0 / padded_len
    alternate = jnp.where(dev_ids % 2 == 0, 1.0, -1.0).astype(jnp.float32)
    cos_half, sin_half = angle_table(dev_ids, dev_ids, freq_count)
    sin_half = jnp.where(dev_ids[:, None] == 0, -alternate[None, :], sin_half)
    twid_half_cos = twid_cos[:seq_count]
    twid_half_sin = twid_sin[:seq_count]
    spread = [
        first_section(piece, cos_half, sin_half, twid_half_cos, twid_half_sin) for piece in received
    ]
    exchanged = (
        lax.all_to_all(spread[0][0], "seq", split_axis=0, concat_axis=1, tiled=True),
        lax.all_to_all(spread[0][1], "seq", split_axis=0, concat_axis=1, tiled=True),
        lax.all_to_all(spread[1][0], "seq", split_axis=0, concat_axis=1, tiled=True),
        lax.all_to_all(spread[1][1], "seq", split_axis=0, concat_axis=1, tiled=True),
        lax.all_to_all(spread[2][0], "seq", split_axis=0, concat_axis=1, tiled=True),
        lax.all_to_all(spread[2][1], "seq", split_axis=0, concat_axis=1, tiled=True),
    )
    corr_real, corr_imag, lag_real, lag_imag = lax.cond(
        seq_place == 0, paired, inverted, tuple(exchanged)
    )
    corr_real, corr_imag, lag_real, lag_imag = (
        lax.all_to_all(corr_real, "seq", split_axis=1, concat_axis=0, tiled=True),
        lax.all_to_all(corr_imag, "seq", split_axis=1, concat_axis=0, tiled=True),
        lax.all_to_all(lag_real, "seq", split_axis=1, concat_axis=0, tiled=True),
        lax.all_to_all(lag_imag, "seq", split_axis=1, concat_axis=0, tiled=True),
    )
    corr_flat_real, corr_flat_imag = rotate_back(
        corr_real.reshape(seq_count, width_all),
        corr_imag.reshape(seq_count, width_all),
        twid_half_cos,
        twid_half_sin,
    )
    lag_flat_real, lag_flat_imag = rotate_back(
        lag_real.reshape(seq_count, width_all),
        lag_imag.reshape(seq_count, width_all),
        twid_half_cos,
        twid_half_sin,
    )
    cos_final, sin_final = angle_table(dev_ids, dev_ids, freq_count)
    cos_final = jnp.where(dev_ids[None, :] == 0, 1.0, 2.0 * cos_final)
    sin_final = jnp.where(dev_ids[None, :] == 0, -alternate[:, None], 2.0 * sin_final)
    conv_rows = (
        matmul_high(cos_final, corr_flat_real) - matmul_high(sin_final, corr_flat_imag)
    ) * scale_term
    lag_rows = (
        matmul_high(cos_final, lag_flat_real) - matmul_high(sin_final, lag_flat_imag)
    ) * scale_term
    conv_back, lag_back = (
        lax.all_to_all(conv_rows, "seq", split_axis=0, concat_axis=0, tiled=True),
        lax.all_to_all(lag_rows, "seq", split_axis=0, concat_axis=0, tiled=True),
    )

    def to_channels(values):
        return (
            values.reshape(seq_count, channels, block_len)
            .transpose(1, 0, 2)
            .reshape(channels, local_len)
        )

    conv_grad = to_channels(conv_back)
    filt_grad = to_channels(lag_back)
    in_grad = conv_grad + local_bias[:, None] * out_grad
    weighted = filt_grad * window
    regrouped = lax.all_to_all(weighted, "ch", split_axis=1, concat_axis=0, tiled=True)
    feat_grad = matmul_high(filter_weight, regrouped)
    return (in_grad, feat_grad)


lanes = 128
lag_joint = 2


def split_table(table):
    table = np.asarray(table, np.float32)
    high_part = table.astype(jnp.bfloat16)
    low_part = (table - high_part.astype(np.float32)).astype(jnp.bfloat16)
    return np.stack([high_part, low_part])


def make_tables(data_rows):
    freq_rows = 2 * data_rows
    padded_len = freq_rows * lanes
    odd_ids = 2 * np.arange(data_rows) + 1
    row_angle = (odd_ids[:, None] * np.arange(data_rows)[None, :] % (2 * freq_rows)) * (
        math.pi / freq_rows
    )
    row_table = np.concatenate([np.cos(row_angle), -np.sin(row_angle)], axis=0)
    lane_ids = np.arange(lanes)
    twist_angle = (odd_ids[:, None] * lane_ids[None, :]) * (math.pi / padded_len)
    twist = np.stack([np.cos(twist_angle), -np.sin(twist_angle)]).astype(np.float32)
    lane_angle = (lane_ids[:, None] * lane_ids[None, :] % lanes) * (2.0 * math.pi / lanes)
    lane_cos, lane_sin = np.cos(lane_angle), np.sin(lane_angle)
    lane_table = np.block([[lane_cos, -lane_sin], [lane_sin, lane_cos]])
    back_table = np.block([[lane_cos, lane_sin], [-lane_sin, lane_cos]]) * (2.0 / padded_len)
    return (
        split_table(row_table),
        split_table(row_table.T),
        split_table(lane_table),
        split_table(back_table),
        twist,
    )


def split_value(value):
    high_part = value.astype(jnp.bfloat16)
    return high_part, (value - high_part.astype(jnp.float32)).astype(jnp.bfloat16)


def dot_split(left, right):
    def product(first, second):
        return jnp.dot(first, second, preferred_element_type=jnp.float32)

    return product(left[0], right[0]) + (product(left[0], right[1]) + product(left[1], right[0]))


def whole_kernel(
    sizes,
    grad_hbm,
    input_hbm,
    feat_hbm,
    weight_ref,
    rate_ref,
    bias_ref,
    row_hbm,
    row_back_hbm,
    lane_hbm,
    lane_back_hbm,
    twist_hbm,
    in_grad_ref,
    feat_grad_ref,
    grad_ref,
    input_ref,
    feat_ref,
    row_ref,
    row_back_ref,
    lane_ref,
    lane_back_ref,
    twist_ref,
    load_sem,
    send_buf,
    gather_buf,
    conv_send,
    lag_send,
    conv_recv,
    lag_recv,
    window_buf,
    rate_buf,
    bias_buf,
    weight_buf,
    fwd_send_sem,
    fwd_recv_sem,
    conv_send_sem,
    conv_recv_sem,
    lag_send_sem,
    lag_recv_sem,
):
    seq_count, ch_count, channels, rows = sizes
    per = channels // seq_count
    joint = math.gcd(per, lag_joint)
    data_rows = rows * seq_count
    sub_rows = rows // ch_count
    all_channels = channels * ch_count
    total = seq_count * ch_count
    full_len = data_rows * lanes
    seq_place = lax.axis_index("seq")
    ch_place = lax.axis_index("ch")
    flat_place = seq_place * ch_count + ch_place

    loads = [
        pltpu.make_async_copy(source, target, load_sem.at[index])
        for index, (source, target) in enumerate(
            (
                (grad_hbm, grad_ref),
                (input_hbm, input_ref),
                (feat_hbm, feat_ref),
                (row_hbm, row_ref),
                (twist_hbm, twist_ref),
                (lane_hbm, lane_ref),
                (lane_back_hbm, lane_back_ref),
                (row_back_hbm, row_back_ref),
            )
        )
    ]
    barrier = pltpu.get_barrier_semaphore()

    def greet(step, carry):
        other = lax.rem(flat_place + step, total)
        pl.semaphore_signal(
            barrier,
            inc=1,
            device_id={"seq": other // ch_count, "ch": lax.rem(other, ch_count)},
            device_id_type=pl.DeviceIdType.MESH,
        )
        return carry

    lax.fori_loop(1, total, greet, 0)
    for load in loads:
        load.start()

    def each_other(place, count, visit):
        def one(step, carry):
            visit(lax.rem(place + step, count))
            return carry

        lax.fori_loop(1, count, one, 0)

    def fwd_copy(which, chan, target, place):
        return pltpu.make_async_remote_copy(
            src_ref=send_buf.at[
                which, pl.ds(pl.multiple_of((target * per + chan) * rows, 8), rows)
            ],
            dst_ref=gather_buf.at[which, chan, pl.ds(pl.multiple_of(place * rows, 8), rows)],
            send_sem=fwd_send_sem.at[which, chan, target],
            recv_sem=fwd_recv_sem.at[which, chan, place],
            device_id={"seq": target, "ch": ch_place},
            device_id_type=pl.DeviceIdType.MESH,
        )

    def conv_copy(chan, target, place):
        return pltpu.make_async_remote_copy(
            src_ref=conv_send.at[chan, pl.ds(pl.multiple_of(target * rows, 8), rows)],
            dst_ref=conv_recv.at[pl.ds(pl.multiple_of((place * per + chan) * rows, 8), rows)],
            send_sem=conv_send_sem.at[chan, target],
            recv_sem=conv_recv_sem.at[chan, place],
            device_id={"seq": target, "ch": ch_place},
            device_id_type=pl.DeviceIdType.MESH,
        )

    def lag_row(flat, chan):
        channel = lax.rem(flat, ch_count) * channels + (flat // ch_count) * per + chan
        return pl.multiple_of(channel * sub_rows, 8)

    def lag_copy(chan, target, flat):
        return pltpu.make_async_remote_copy(
            src_ref=lag_send.at[target, pl.ds(pl.multiple_of(chan * sub_rows, 8), joint * sub_rows)],
            dst_ref=lag_recv.at[pl.ds(lag_row(flat, chan), joint * sub_rows)],
            send_sem=lag_send_sem.at[chan, target],
            recv_sem=lag_recv_sem.at[chan, flat],
            device_id={"seq": target // ch_count, "ch": lax.rem(target, ch_count)},
            device_id_type=pl.DeviceIdType.MESH,
        )

    def to_rows(which, index, tile):
        send_buf[which, pl.ds(index, channels, stride=rows), :] = tile

    rate_buf[...] = jnp.broadcast_to(rate_ref[...], (lanes, all_channels)).T
    weight_buf[...] = weight_ref[...].T
    loads[0].wait()
    for index in range(rows):
        to_rows(0, index, grad_ref[:, index * lanes : (index + 1) * lanes])
    loads[1].wait()
    for index in range(rows):
        to_rows(1, index, input_ref[:, index * lanes : (index + 1) * lanes])

    pl.semaphore_wait(barrier, total - 1)

    def send_fwd(which, chan):
        each_other(
            seq_place,
            seq_count,
            lambda target: fwd_copy(which, chan, target, seq_place).start(),
        )

    send_fwd(0, 0)
    send_fwd(1, 0)

    first_chan = pl.multiple_of(ch_place * channels, 8)
    local_rates = rate_buf[pl.ds(first_chan, channels), :]
    local_weight = split_value(weight_buf[pl.ds(first_chan, channels), :])
    lane_ids = lax.broadcasted_iota(jnp.int32, (1, lanes), 1)

    def window_of(rates, first):
        steps_t = (first + lane_ids).astype(jnp.float32) / full_len
        return jnp.exp(-rates * steps_t) + shift_term

    bias_buf[...] = jnp.broadcast_to(bias_ref[...], (lanes, all_channels)).T
    loads[2].wait()
    chunk = math.gcd(rows, 4)
    for outer in range(rows // chunk):
        lo = outer * chunk * lanes
        block = split_value(feat_ref[:, lo : lo + chunk * lanes])
        values = dot_split(local_weight, block)
        for inner in range(chunk):
            index = outer * chunk + inner
            window = window_of(local_rates, (seq_place * rows + index) * lanes)
            to_rows(2, index, values[:, inner * lanes : (inner + 1) * lanes] * window)

    send_fwd(2, 0)

    def send_rest(chan, carry):
        for which in range(3):
            send_fwd(which, chan)
        return carry

    lax.fori_loop(1, per, send_rest, 0)

    own_rows = pl.ds(pl.multiple_of(seq_place * rows, 8), rows)

    def keep_own(chan, carry):
        for which in range(3):
            gather_buf[which, chan, own_rows, :] = send_buf[
                which, pl.ds(pl.multiple_of((seq_place * per + chan) * rows, 8), rows), :
            ]
        return carry

    lax.fori_loop(0, per, keep_own, 0)

    for index in range(sub_rows):
        window_buf[index] = window_of(rate_buf[...], (flat_place * sub_rows + index) * lanes)

    for load in loads[3:]:
        load.wait()

    def work(chan, carry):
        def arrive(source):
            for which in range(3):
                fwd_copy(which, chan, source, source).wait_recv()

        each_other(seq_place, seq_count, arrive)

        twist_cos, twist_sin = twist_ref[0], twist_ref[1]
        packed = jnp.concatenate([gather_buf[which, chan] for which in range(3)], axis=1)
        spread = dot_split((row_ref[0], row_ref[1]), split_value(packed))
        turned = []
        for which in range(3):
            re_part = spread[:data_rows, which * lanes : (which + 1) * lanes]
            im_part = spread[data_rows:, which * lanes : (which + 1) * lanes]
            turned.append(
                jnp.concatenate(
                    [
                        re_part * twist_cos - im_part * twist_sin,
                        re_part * twist_sin + im_part * twist_cos,
                    ],
                    axis=1,
                )
            )
        freqs = [
            dot_split(split_value(part), (lane_ref[0], lane_ref[1])) for part in turned
        ]
        grad_re, grad_im = freqs[0][:, :lanes], freqs[0][:, lanes:]

        def inverse(spectrum):
            re_part, im_part = spectrum[:, :lanes], spectrum[:, lanes:]
            product = jnp.concatenate(
                [
                    re_part * grad_re + im_part * grad_im,
                    re_part * grad_im - im_part * grad_re,
                ],
                axis=1,
            )
            back = dot_split(split_value(product), (lane_back_ref[0], lane_back_ref[1]))
            re_part, im_part = back[:, :lanes], back[:, lanes:]
            return jnp.concatenate(
                [
                    re_part * twist_cos + im_part * twist_sin,
                    im_part * twist_cos - re_part * twist_sin,
                ],
                axis=0,
            )

        both = jnp.concatenate([inverse(freqs[2]), inverse(freqs[1])], axis=1)
        final = dot_split((row_back_ref[0], row_back_ref[1]), split_value(both))
        conv_send[chan] = final[:, :lanes]
        lag_send[:, pl.ds(pl.multiple_of(chan * sub_rows, 8), sub_rows), :] = final[
            :, lanes:
        ].reshape(total, sub_rows, lanes)

        @pl.when(lax.rem(chan, joint) == joint - 1)
        def _():
            each_other(
                flat_place,
                total,
                lambda target: lag_copy(chan - (joint - 1), target, flat_place).start(),
            )

        each_other(
            seq_place, seq_count, lambda target: conv_copy(chan, target, seq_place).start()
        )
        conv_recv[
            pl.ds(pl.multiple_of((seq_place * per + chan) * rows, 8), rows), :
        ] = conv_send[chan, own_rows, :]
        lag_recv[pl.ds(lag_row(flat_place, chan), sub_rows), :] = lag_send[
            flat_place, pl.ds(pl.multiple_of(chan * sub_rows, 8), sub_rows), :
        ]
        return carry

    lax.fori_loop(0, per, work, 0)

    def fwd_sent(chan, carry):
        def one(target):
            for which in range(3):
                fwd_copy(which, chan, target, seq_place).wait_send()

        each_other(seq_place, seq_count, one)
        return carry

    def conv_sent(chan, carry):
        each_other(
            seq_place,
            seq_count,
            lambda target: conv_copy(chan, target, seq_place).wait_send(),
        )
        return carry

    def conv_arrive(chan, carry):
        each_other(
            seq_place, seq_count, lambda source: conv_copy(chan, source, source).wait_recv()
        )
        return carry

    def lag_sent(group, carry):
        each_other(
            flat_place,
            total,
            lambda target: lag_copy(group * joint, target, flat_place).wait_send(),
        )
        return carry

    def lag_arrive(group, carry):
        each_other(
            flat_place,
            total,
            lambda source: lag_copy(group * joint, source, source).wait_recv(),
        )
        return carry

    last_group = per // joint - 1
    lax.fori_loop(0, per, fwd_sent, 0)
    lax.fori_loop(0, last_group, lag_sent, 0)
    lax.fori_loop(0, per - 1, conv_sent, 0)
    lax.fori_loop(0, last_group, lag_arrive, 0)
    lax.fori_loop(0, per - 1, conv_arrive, 0)
    lax.fori_loop(last_group, per // joint, lag_sent, 0)
    lax.fori_loop(last_group, per // joint, lag_arrive, 0)
    weight = split_value(weight_ref[...])
    for index in range(sub_rows):
        tile = lag_recv[pl.ds(index, all_channels, stride=sub_rows), :] * window_buf[index]
        feat_grad_ref[:, index * lanes : (index + 1) * lanes] = dot_split(
            weight, split_value(tile)
        )

    lax.fori_loop(per - 1, per, conv_sent, 0)
    lax.fori_loop(per - 1, per, conv_arrive, 0)
    local_bias = bias_buf[pl.ds(first_chan, channels), :]
    for index in range(rows):
        span = slice(index * lanes, (index + 1) * lanes)
        in_grad_ref[:, span] = (
            conv_recv[pl.ds(index, channels, stride=rows), :] + local_bias * grad_ref[:, span]
        )


def local_whole(seq_count, ch_count, tables, *args):
    out_grad, gated_input, features, filter_weight, rates, skip_bias = args
    channels, local_len = out_grad.shape
    rows = local_len // lanes
    feats, all_channels = filter_weight.shape
    per = channels // seq_count
    data_rows = rows * seq_count
    sub_rows = rows // ch_count
    total = seq_count * ch_count
    sizes = (seq_count, ch_count, channels, rows)
    in_vmem = pl.BlockSpec(memory_space=pltpu.VMEM)
    anywhere = pl.BlockSpec(memory_space=pl.ANY)
    dma = pltpu.SemaphoreType.DMA
    f32 = jnp.float32
    return pl.pallas_call(
        functools.partial(whole_kernel, sizes),
        out_shape=(
            jax.ShapeDtypeStruct((channels, local_len), f32),
            jax.ShapeDtypeStruct((feats, sub_rows * lanes), f32),
        ),
        in_specs=[anywhere] * 3 + [in_vmem] * 3 + [anywhere] * 5,
        out_specs=(in_vmem, in_vmem),
        scratch_shapes=[
            pltpu.VMEM((channels, local_len), f32),
            pltpu.VMEM((channels, local_len), f32),
            pltpu.VMEM((feats, local_len), f32),
            *[pltpu.VMEM(table.shape, table.dtype) for table in tables],
            dma((8,)),
            pltpu.VMEM((3, channels * rows, lanes), f32),
            pltpu.VMEM((3, per, data_rows, lanes), f32),
            pltpu.VMEM((per, data_rows, lanes), f32),
            pltpu.VMEM((total, per * sub_rows, lanes), f32),
            pltpu.VMEM((channels * rows, lanes), f32),
            pltpu.VMEM((all_channels * sub_rows, lanes), f32),
            pltpu.VMEM((sub_rows, all_channels, lanes), f32),
            pltpu.VMEM((all_channels, lanes), f32),
            pltpu.VMEM((all_channels, lanes), f32),
            pltpu.VMEM((all_channels, feats), f32),
            dma((3, per, seq_count)),
            dma((3, per, seq_count)),
            dma((per, seq_count)),
            dma((per, seq_count)),
            dma((per, total)),
            dma((per, total)),
        ],
        compiler_params=pltpu.CompilerParams(collective_id=0, has_side_effects=True),
    )(
        out_grad,
        gated_input,
        features,
        filter_weight,
        rates.reshape(1, all_channels),
        skip_bias.reshape(1, all_channels),
        *[jnp.asarray(table) for table in tables],
    )


def solution(mesh):
    seq_count, ch_count = mesh.shape["seq"], mesh.shape["ch"]
    in_specs = (P("ch", "seq"), P("ch", "seq"), P(None, "seq"), P(), P(), P())
    out_specs = (P("ch", "seq"), P(None, ("seq", "ch")))

    def whole(*args):
        channels, full_len = args[0].shape
        channels = channels // ch_count
        local_len = full_len // seq_count
        fits = (
            seq_count % 2 == 0
            and channels % seq_count == 0
            and channels % 8 == 0
            and local_len % (8 * lanes * ch_count) == 0
            and full_len <= 512 * lanes
        )
        body = local
        if fits:
            tables = make_tables(full_len // lanes)
            body = functools.partial(local_whole, seq_count, ch_count, tables)
        return jax.shard_map(
            body, mesh=mesh, in_specs=in_specs, out_specs=out_specs, check_vma=False
        )(*args)

    return whole
```

profile of v0, /device:TPU:0, one launch (start us, length us, event | category | flops | bytes accessed | tf_op | source)
XLA Modules:
  0.0 74.1 jit_solution(11299801147940757327)
XLA Ops:
  0.6 70.8 %shard_map.122 = (f32[32,4096]{1,0:T(8,128)}, f32[64,1024]{1,0:T(8,128)}) custom-call(f32[32,4096]{1,0:T(8,128)} %grad_hbm.1, f32[32,4096]{1,0:T(8,128)} %input_hbm.1, f32[64,4096]{1,0:T(8,128)} %feat_hbm.1, f32[64,128]{1,0:T(8,128)} %weight_ref.1, f32[1,128]{1,0:T(1,128)} %bitcast.2, f32[1,128]{1,0:T(1,128)} %bitcast.3, ...), custom_call_target="tpu_custom_call" | custom-call | tf_op jit(solution)/shard_map/pallas_call | solution.py:670
  71.5 0.0 copy-start
  71.5 1.9 %copy.15 = f32[32,4096]{1,0:T(8,128)} copy(f32[32,4096]{1,0:T(8,128)} %get-tuple-element.4) | data formatting | bytes 1048576
  73.4 0.0 copy-done
  73.4 0.7 copy.16
Async XLA Ops:
  71.5 1.9 %copy-start = (f32[64,1024]{1,0:T(8,128)S(1)}, f32[64,1024]{1,0:T(8,128)}, u32[]{:S(2)}) copy-start(f32[64,1024]{1,0:T(8,128)} %get-tuple-element.5) | copy-start | bytes 786436
where the time goes:
time: 74.3 us; the launch traced here: 74.1 us
  Pallas kernels  70.8 us (95%)
  local copies, waits for them, and re-layouts  2.62 us (4%)
    pallas_call x1, Pallas kernels, local_whole(): pl.pallas_call(functools.partial(whole_kernel, sizes), out_shape=(jax.Sha...  70.8 us
    unnamed x4, local copies, waits for them, and re-layouts  2.62 us

commit v1 on v0

--- a/solution.py
+++ b/solution.py
@@ -271,7 +271,7 @@
 
 
 lanes = 128
-lag_joint = 2
+conv_joint = 2
 
 
 def split_table(table):
@@ -330,8 +330,8 @@
     lane_hbm,
     lane_back_hbm,
     twist_hbm,
-    in_grad_ref,
-    feat_grad_ref,
+    in_grad_hbm,
+    feat_grad_hbm,
     grad_ref,
     input_ref,
     feat_ref,
@@ -341,6 +341,8 @@
     lane_back_ref,
     twist_ref,
     load_sem,
+    in_grad_ref,
+    feat_grad_ref,
     send_buf,
     gather_buf,
     conv_send,
@@ -351,16 +353,15 @@
     rate_buf,
     bias_buf,
     weight_buf,
-    fwd_send_sem,
     fwd_recv_sem,
-    conv_send_sem,
     conv_recv_sem,
-    lag_send_sem,
+    send_sem,
     lag_recv_sem,
+    store_sem,
 ):
     seq_count, ch_count, channels, rows = sizes
     per = channels // seq_count
-    joint = math.gcd(per, lag_joint)
+    joint = math.gcd(per, conv_joint)
     data_rows = rows * seq_count
     sub_rows = rows // ch_count
     all_channels = channels * ch_count
@@ -408,40 +409,59 @@
 
         lax.fori_loop(1, count, one, 0)
 
-    def fwd_copy(which, chan, target, place):
+    def remote(source, target, send, recv, device):
         return pltpu.make_async_remote_copy(
-            src_ref=send_buf.at[
-                which, pl.ds(pl.multiple_of((target * per + chan) * rows, 8), rows)
+            src_ref=source,
+            dst_ref=target,
+            send_sem=send,
+            recv_sem=recv,
+            device_id=device,
+            device_id_type=pl.DeviceIdType.MESH,
+        )
+
+    def fwd_copy(first, last, chan, target):
+        return remote(
+            send_buf.at[
+                first:last, pl.ds(pl.multiple_of((target * per + chan) * rows, 8), rows)
             ],
-            dst_ref=gather_buf.at[which, chan, pl.ds(pl.multiple_of(place * rows, 8), rows)],
-            send_sem=fwd_send_sem.at[which, chan, target],
-            recv_sem=fwd_recv_sem.at[which, chan, place],
-            device_id={"seq": target, "ch": ch_place},
-            device_id_type=pl.DeviceIdType.MESH,
-        )
-
-    def conv_copy(chan, target, place):
-        return pltpu.make_async_remote_copy(
-            src_ref=conv_send.at[chan, pl.ds(pl.multiple_of(target * rows, 8), rows)],
-            dst_ref=conv_recv.at[pl.ds(pl.multiple_of((place * per + chan) * rows, 8), rows)],
-            send_sem=conv_send_sem.at[chan, target],
-            recv_sem=conv_recv_sem.at[chan, place],
-            device_id={"seq": target, "ch": ch_place},
-            device_id_type=pl.DeviceIdType.MESH,
-        )
-
-    def lag_row(flat, chan):
-        channel = lax.rem(flat, ch_count) * channels + (flat // ch_count) * per + chan
+            gather_buf.at[
+                first:last, chan, pl.ds(pl.multiple_of(seq_place * rows, 8), rows)
+            ],
+            send_sem.at[0],
+            fwd_recv_sem.at[chan],
+            {"seq": target, "ch": ch_place},
+        )
+
+    def fwd_arrived(chan):
+        part = gather_buf.at[:, chan, pl.ds(0, (seq_count - 1) * rows)]
+        remote(
+            part, part, send_sem.at[0], fwd_recv_sem.at[chan], {"seq": seq_place, "ch": ch_place}
+        ).wait_recv()
+
+    def conv_copy(group, target):
+        return remote(
+            conv_send.at[target, pl.ds(pl.multiple_of(group * joint * rows, 8), joint * rows)],
+            conv_recv.at[
+                pl.ds(
+                    pl.multiple_of((seq_place * per + group * joint) * rows, 8), joint * rows
+                )
+            ],
+            send_sem.at[1],
+            conv_recv_sem.at[group],
+            {"seq": target, "ch": ch_place},
+        )
+
+    def lag_row(flat):
+        channel = lax.rem(flat, ch_count) * channels + (flat // ch_count) * per
         return pl.multiple_of(channel * sub_rows, 8)
 
-    def lag_copy(chan, target, flat):
-        return pltpu.make_async_remote_copy(
-            src_ref=lag_send.at[target, pl.ds(pl.multiple_of(chan * sub_rows, 8), joint * sub_rows)],
-            dst_ref=lag_recv.at[pl.ds(lag_row(flat, chan), joint * sub_rows)],
-            send_sem=lag_send_sem.at[chan, target],
-            recv_sem=lag_recv_sem.at[chan, flat],
-            device_id={"seq": target // ch_count, "ch": lax.rem(target, ch_count)},
-            device_id_type=pl.DeviceIdType.MESH,
+    def lag_copy(target):
+        return remote(
+            lag_send.at[target],
+            lag_recv.at[pl.ds(lag_row(flat_place), per * sub_rows)],
+            send_sem.at[2],
+            lag_recv_sem.at[0],
+            {"seq": target // ch_count, "ch": lax.rem(target, ch_count)},
         )
 
     def to_rows(which, index, tile):
@@ -458,15 +478,12 @@
 
     pl.semaphore_wait(barrier, total - 1)
 
-    def send_fwd(which, chan):
+    def send_fwd(first, last, chan):
         each_other(
-            seq_place,
-            seq_count,
-            lambda target: fwd_copy(which, chan, target, seq_place).start(),
-        )
-
-    send_fwd(0, 0)
-    send_fwd(1, 0)
+            seq_place, seq_count, lambda target: fwd_copy(first, last, chan, target).start()
+        )
+
+    send_fwd(0, 2, 0)
 
     first_chan = pl.multiple_of(ch_place * channels, 8)
     local_rates = rate_buf[pl.ds(first_chan, channels), :]
@@ -489,11 +506,10 @@
             window = window_of(local_rates, (seq_place * rows + index) * lanes)
             to_rows(2, index, values[:, inner * lanes : (inner + 1) * lanes] * window)
 
-    send_fwd(2, 0)
+    send_fwd(2, 3, 0)
 
     def send_rest(chan, carry):
-        for which in range(3):
-            send_fwd(which, chan)
+        send_fwd(0, 3, chan)
         return carry
 
     lax.fori_loop(1, per, send_rest, 0)
@@ -516,11 +532,7 @@
         load.wait()
 
     def work(chan, carry):
-        def arrive(source):
-            for which in range(3):
-                fwd_copy(which, chan, source, source).wait_recv()
-
-        each_other(seq_place, seq_count, arrive)
+        fwd_arrived(chan)
 
         twist_cos, twist_sin = twist_ref[0], twist_ref[1]
         packed = jnp.concatenate([gather_buf[which, chan] for which in range(3)], axis=1)
@@ -564,93 +576,57 @@
 
         both = jnp.concatenate([inverse(freqs[2]), inverse(freqs[1])], axis=1)
         final = dot_split((row_back_ref[0], row_back_ref[1]), split_value(both))
-        conv_send[chan] = final[:, :lanes]
+        conv_send[:, pl.ds(pl.multiple_of(chan * rows, 8), rows), :] = final[:, :lanes].reshape(
+            seq_count, rows, lanes
+        )
         lag_send[:, pl.ds(pl.multiple_of(chan * sub_rows, 8), sub_rows), :] = final[
             :, lanes:
         ].reshape(total, sub_rows, lanes)
 
         @pl.when(lax.rem(chan, joint) == joint - 1)
         def _():
-            each_other(
-                flat_place,
-                total,
-                lambda target: lag_copy(chan - (joint - 1), target, flat_place).start(),
-            )
-
-        each_other(
-            seq_place, seq_count, lambda target: conv_copy(chan, target, seq_place).start()
-        )
-        conv_recv[
-            pl.ds(pl.multiple_of((seq_place * per + chan) * rows, 8), rows), :
-        ] = conv_send[chan, own_rows, :]
-        lag_recv[pl.ds(lag_row(flat_place, chan), sub_rows), :] = lag_send[
-            flat_place, pl.ds(pl.multiple_of(chan * sub_rows, 8), sub_rows), :
-        ]
+            group = chan // joint
+            each_other(seq_place, seq_count, lambda target: conv_copy(group, target).start())
+
         return carry
 
     lax.fori_loop(0, per, work, 0)
-
-    def fwd_sent(chan, carry):
-        def one(target):
-            for which in range(3):
-                fwd_copy(which, chan, target, seq_place).wait_send()
-
-        each_other(seq_place, seq_count, one)
-        return carry
-
-    def conv_sent(chan, carry):
-        each_other(
-            seq_place,
-            seq_count,
-            lambda target: conv_copy(chan, target, seq_place).wait_send(),
-        )
-        return carry
-
-    def conv_arrive(chan, carry):
-        each_other(
-            seq_place, seq_count, lambda source: conv_copy(chan, source, source).wait_recv()
-        )
-        return carry
-
-    def lag_sent(group, carry):
-        each_other(
-            flat_place,
-            total,
-            lambda target: lag_copy(group * joint, target, flat_place).wait_send(),
-        )
-        return carry
-
-    def lag_arrive(group, carry):
-        each_other(
-            flat_place,
-            total,
-            lambda source: lag_copy(group * joint, source, source).wait_recv(),
-        )
-        return carry
-
-    last_group = per // joint - 1
-    lax.fori_loop(0, per, fwd_sent, 0)
-    lax.fori_loop(0, last_group, lag_sent, 0)
-    lax.fori_loop(0, per - 1, conv_sent, 0)
-    lax.fori_loop(0, last_group, lag_arrive, 0)
-    lax.fori_loop(0, per - 1, conv_arrive, 0)
-    lax.fori_loop(last_group, per // joint, lag_sent, 0)
-    lax.fori_loop(last_group, per // joint, lag_arrive, 0)
+    each_other(flat_place, total, lambda target: lag_copy(target).start())
+    conv_recv[pl.ds(pl.multiple_of(seq_place * per * rows, 8), per * rows), :] = conv_send[
+        seq_place
+    ]
+    lag_recv[pl.ds(lag_row(flat_place), per * sub_rows), :] = lag_send[flat_place]
+
+    here = {"seq": seq_place, "ch": ch_place}
+    for group in range(per // joint):
+        part = conv_recv.at[pl.ds(0, (seq_count - 1) * joint * rows)]
+        remote(part, part, send_sem.at[1], conv_recv_sem.at[group], here).wait_recv()
+    local_bias = bias_buf[pl.ds(first_chan, channels), :]
+    for index in range(rows):
+        span = slice(index * lanes, (index + 1) * lanes)
+        in_grad_ref[:, span] = (
+            conv_recv[pl.ds(index, channels, stride=rows), :] + local_bias * grad_ref[:, span]
+        )
+    in_grad_store = pltpu.make_async_copy(in_grad_ref, in_grad_hbm, store_sem.at[0])
+    in_grad_store.start()
+
+    part = send_buf.at[:, pl.ds(0, (seq_count - 1) * per * rows)]
+    remote(part, part, send_sem.at[0], fwd_recv_sem.at[0], here).wait_send()
+    part = conv_recv.at[pl.ds(0, (seq_count - 1) * per * rows)]
+    remote(part, part, send_sem.at[1], conv_recv_sem.at[0], here).wait_send()
+    part = lag_send.at[pl.ds(0, total - 1)]
+    remote(part, part, send_sem.at[2], lag_recv_sem.at[0], here).wait_send()
+    remote(part, part, send_sem.at[2], lag_recv_sem.at[0], here).wait_recv()
     weight = split_value(weight_ref[...])
     for index in range(sub_rows):
         tile = lag_recv[pl.ds(index, all_channels, stride=sub_rows), :] * window_buf[index]
         feat_grad_ref[:, index * lanes : (index + 1) * lanes] = dot_split(
             weight, split_value(tile)
         )
-
-    lax.fori_loop(per - 1, per, conv_sent, 0)
-    lax.fori_loop(per - 1, per, conv_arrive, 0)
-    local_bias = bias_buf[pl.ds(first_chan, channels), :]
-    for index in range(rows):
-        span = slice(index * lanes, (index + 1) * lanes)
-        in_grad_ref[:, span] = (
-            conv_recv[pl.ds(index, channels, stride=rows), :] + local_bias * grad_ref[:, span]
-        )
+    feat_store = pltpu.make_async_copy(feat_grad_ref, feat_grad_hbm, store_sem.at[1])
+    feat_store.start()
+    in_grad_store.wait()
+    feat_store.wait()
 
 
 def local_whole(seq_count, ch_count, tables, *args):
@@ -674,16 +650,18 @@
             jax.ShapeDtypeStruct((feats, sub_rows * lanes), f32),
         ),
         in_specs=[anywhere] * 3 + [in_vmem] * 3 + [anywhere] * 5,
-        out_specs=(in_vmem, in_vmem),
+        out_specs=(anywhere, anywhere),
         scratch_shapes=[
             pltpu.VMEM((channels, local_len), f32),
             pltpu.VMEM((channels, local_len), f32),
             pltpu.VMEM((feats, local_len), f32),
             *[pltpu.VMEM(table.shape, table.dtype) for table in tables],
             dma((8,)),
+            pltpu.VMEM((channels, local_len), f32),
+            pltpu.VMEM((feats, sub_rows * lanes), f32),
             pltpu.VMEM((3, channels * rows, lanes), f32),
             pltpu.VMEM((3, per, data_rows, lanes), f32),
-            pltpu.VMEM((per, data_rows, lanes), f32),
+            pltpu.VMEM((seq_count, per * rows, lanes), f32),
             pltpu.VMEM((total, per * sub_rows, lanes), f32),
             pltpu.VMEM((channels * rows, lanes), f32),
             pltpu.VMEM((all_channels * sub_rows, lanes), f32),
@@ -691,12 +669,11 @@
             pltpu.VMEM((all_channels, lanes), f32),
             pltpu.VMEM((all_channels, lanes), f32),
             pltpu.VMEM((all_channels, feats), f32),
-            dma((3, per, seq_count)),
-            dma((3, per, seq_count)),
-            dma((per, seq_count)),
-            dma((per, seq_count)),
-            dma((per, total)),
-            dma((per, total)),
+            dma((per,)),
+            dma((per // math.gcd(per, conv_joint),)),
+            dma((3,)),
+            dma((1,)),
+            dma((2,)),
         ],
         compiler_params=pltpu.CompilerParams(collective_id=0, has_side_effects=True),
     )(

time: 74.3 us -> 67.8 us (0.913)
  the two profiles are of different devices: /device:TPU:0 before, /device:TPU:15 now
where the time goes in v1:
time: 67.8 us; the launch traced here: 67.6 us
  Pallas kernels  64.4 us (95%)
  local copies, waits for them, and re-layouts  2.62 us (4%)
    pallas_call x1, Pallas kernels, local_whole(): pl.pallas_call(functools.partial(whole_kernel, sizes), out_shape=(jax.Sha...  64.4 us
    unnamed x4, local copies, waits for them, and re-layouts  2.62 us

profile of v1, /device:TPU:15, one launch (start us, length us, event | category | flops | bytes accessed | tf_op | source)
XLA Modules:
  0.0 67.6 jit_solution(3005528830077201083)
XLA Ops:
  0.6 64.4 %shard_map.122 = (f32[32,4096]{1,0:T(8,128)}, f32[64,1024]{1,0:T(8,128)}) custom-call(f32[32,4096]{1,0:T(8,128)} %grad_hbm.1, f32[32,4096]{1,0:T(8,128)} %input_hbm.1, f32[64,4096]{1,0:T(8,128)} %feat_hbm.1, f32[64,128]{1,0:T(8,128)} %weight_ref.1, f32[1,128]{1,0:T(1,128)} %bitcast.2, f32[1,128]{1,0:T(1,128)} %bitcast.3, ...), custom_call_target="tpu_custom_call" | custom-call | tf_op jit(solution)/shard_map/pallas_call | solution.py:646
  65.0 0.0 copy-start
  65.0 1.9 %copy.15 = f32[32,4096]{1,0:T(8,128)} copy(f32[32,4096]{1,0:T(8,128)} %get-tuple-element.4) | data formatting | bytes 1048576
  66.9 0.0 copy-done
  66.9 0.7 %copy.16 = f32[64,1024]{1,0:T(8,128)} copy(f32[64,1024]{1,0:T(8,128)S(1)} %copy-done) | data formatting | bytes 524288
Async XLA Ops:
  65.0 1.9 %copy-start = (f32[64,1024]{1,0:T(8,128)S(1)}, f32[64,1024]{1,0:T(8,128)}, u32[]{:S(2)}) copy-start(f32[64,1024]{1,0:T(8,128)} %get-tuple-element.5) | copy-start | bytes 786436

commit v2 on v1

--- a/solution.py
+++ b/solution.py
@@ -271,7 +271,6 @@
 
 
 lanes = 128
-conv_joint = 2
 
 
 def split_table(table):
@@ -317,59 +316,119 @@
     return product(left[0], right[0]) + (product(left[0], right[1]) + product(left[1], right[0]))
 
 
-def whole_kernel(
-    sizes,
-    grad_hbm,
-    input_hbm,
-    feat_hbm,
-    weight_ref,
-    rate_ref,
-    bias_ref,
-    row_hbm,
-    row_back_hbm,
-    lane_hbm,
-    lane_back_hbm,
-    twist_hbm,
-    in_grad_hbm,
-    feat_grad_hbm,
-    grad_ref,
-    input_ref,
-    feat_ref,
-    row_ref,
-    row_back_ref,
-    lane_ref,
-    lane_back_ref,
-    twist_ref,
-    load_sem,
-    in_grad_ref,
-    feat_grad_ref,
-    send_buf,
-    gather_buf,
-    conv_send,
-    lag_send,
-    conv_recv,
-    lag_recv,
-    window_buf,
-    rate_buf,
-    bias_buf,
-    weight_buf,
-    fwd_recv_sem,
-    conv_recv_sem,
-    send_sem,
-    lag_recv_sem,
-    store_sem,
-):
+def correlate(pieces, row_ref, row_back_ref, lane_ref, lane_back_ref, twist_ref):
+    data_rows = pieces[0].shape[0]
+    twist_cos, twist_sin = twist_ref[0], twist_ref[1]
+    packed = jnp.concatenate(pieces, axis=1)
+    spread = dot_split((row_ref[0], row_ref[1]), split_value(packed))
+    freqs = []
+    for which in range(3):
+        re_part = spread[:data_rows, which * lanes : (which + 1) * lanes]
+        im_part = spread[data_rows:, which * lanes : (which + 1) * lanes]
+        turned = jnp.concatenate(
+            [
+                re_part * twist_cos - im_part * twist_sin,
+                re_part * twist_sin + im_part * twist_cos,
+            ],
+            axis=1,
+        )
+        freqs.append(dot_split(split_value(turned), (lane_ref[0], lane_ref[1])))
+    grad_re, grad_im = freqs[0][:, :lanes], freqs[0][:, lanes:]
+
+    def inverse(spectrum):
+        re_part, im_part = spectrum[:, :lanes], spectrum[:, lanes:]
+        product = jnp.concatenate(
+            [
+                re_part * grad_re + im_part * grad_im,
+                re_part * grad_im - im_part * grad_re,
+            ],
+            axis=1,
+        )
+        back = dot_split(split_value(product), (lane_back_ref[0], lane_back_ref[1]))
+        re_part, im_part = back[:, :lanes], back[:, lanes:]
+        return jnp.concatenate(
+            [
+                re_part * twist_cos + im_part * twist_sin,
+                im_part * twist_cos - re_part * twist_sin,
+            ],
+            axis=0,
+        )
+
+    both = jnp.concatenate([inverse(freqs[2]), inverse(freqs[1])], axis=1)
+    return dot_split((row_back_ref[0], row_back_ref[1]), split_value(both))
+
+
+def plan(seq_count, channels):
+    half = seq_count // 2
+    mixed = channels // 8
+    inner = half // 2
+    return half, inner, mixed, mixed // max(inner, 1), (channels - mixed) // half
+
+
+def whole_kernel(sizes, *refs):
+    (
+        grad_hbm,
+        input_hbm,
+        feat_hbm,
+        weight_ref,
+        rate_ref,
+        bias_ref,
+        row_hbm,
+        row_back_hbm,
+        lane_hbm,
+        lane_back_hbm,
+        twist_hbm,
+        half_row_hbm,
+        half_back_hbm,
+        half_twist_hbm,
+        in_grad_ref,
+        feat_grad_ref,
+        grad_ref,
+        input_ref,
+        feat_ref,
+        row_ref,
+        row_back_ref,
+        lane_ref,
+        lane_back_ref,
+        twist_ref,
+        half_row_ref,
+        half_back_ref,
+        half_twist_ref,
+        load_sem,
+        send_buf,
+        gather_full,
+        gather_half,
+        conv_send,
+        lag_send,
+        conv_recv,
+        lag_recv,
+        window_buf,
+        rate_buf,
+        bias_buf,
+        weight_buf,
+        ruler,
+        full_sem,
+        half_sem,
+        send_sem,
+        back_sem,
+    ) = refs
     seq_count, ch_count, channels, rows = sizes
-    per = channels // seq_count
-    joint = math.gcd(per, conv_joint)
+    half, inner, mixed, mixed_per, per = plan(seq_count, channels)
     data_rows = rows * seq_count
     sub_rows = rows // ch_count
     all_channels = channels * ch_count
     total = seq_count * ch_count
+    left_total = half * ch_count
     full_len = data_rows * lanes
     seq_place = lax.axis_index("seq")
     ch_place = lax.axis_index("ch")
     flat_place = seq_place * ch_count + ch_place
+    on_right = seq_place >= half
+    on_left = seq_place < half
+    on_inner = jnp.logical_and(seq_place >= inner, on_left)
+    on_outer = seq_place < inner
+    side_place = lax.rem(seq_place, half)
+    here = {"seq": seq_place, "ch": ch_place}
 
     loads = [
         pltpu.make_async_copy(source, target, load_sem.at[index])
@@ -383,6 +442,9 @@
                 (lane_hbm, lane_ref),
                 (lane_back_hbm, lane_back_ref),
                 (row_back_hbm, row_back_ref),
+                (half_row_hbm, half_row_ref),
+                (half_back_hbm, half_back_ref),
+                (half_twist_hbm, half_twist_ref),
             )
         )
     ]
@@ -402,12 +464,12 @@
     for load in loads:
         load.start()
 
-    def each_other(place, count, visit):
+    def each_other(place, count, visit, first=1):
         def one(step, carry):
             visit(lax.rem(place + step, count))
             return carry
 
-        lax.fori_loop(1, count, one, 0)
+        lax.fori_loop(first, count, one, 0)
 
     def remote(source, target, send, recv, device):
         return pltpu.make_async_remote_copy(
@@ -419,48 +481,94 @@
             device_id_type=pl.DeviceIdType.MESH,
         )
 
-    def fwd_copy(first, last, chan, target):
+    def counted(count, send, recv):
+        part = ruler.at[pl.ds(0, count)]
+        return remote(part, part, send, recv, here)
+
+    def rows_of(channel):
+        return pl.ds(pl.multiple_of(channel * rows, 8), rows)
+
+    def split_channel(side, chan):
+        return mixed + side * per + chan
+
+    def full_copy(first, last, channel, slot, target, sem):
         return remote(
-            send_buf.at[
-                first:last, pl.ds(pl.multiple_of((target * per + chan) * rows, 8), rows)
-            ],
-            gather_buf.at[
-                first:last, chan, pl.ds(pl.multiple_of(seq_place * rows, 8), rows)
-            ],
-            send_sem.at[0],
-            fwd_recv_sem.at[chan],
+            send_buf.at[first:last, rows_of(channel)],
+            gather_full.at[first:last, slot, rows_of(seq_place)],
+            send_sem.at[sem],
+            full_sem.at[slot],
             {"seq": target, "ch": ch_place},
         )
 
-    def fwd_arrived(chan):
-        part = gather_buf.at[:, chan, pl.ds(0, (seq_count - 1) * rows)]
-        remote(
-            part, part, send_sem.at[0], fwd_recv_sem.at[chan], {"seq": seq_place, "ch": ch_place}
-        ).wait_recv()
-
-    def conv_copy(group, target):
+    def half_copy(first, last, channel, slot, target):
         return remote(
-            conv_send.at[target, pl.ds(pl.multiple_of(group * joint * rows, 8), joint * rows)],
-            conv_recv.at[
+            send_buf.at[first:last, rows_of(channel)],
+            gather_half.at[first:last, slot, rows_of(side_place)],
+            send_sem.at[1],
+            half_sem.at[slot],
+            {"seq": target, "ch": ch_place},
+        )
+
+    def send_mixed(first, last):
+        for side in range(inner):
+            target = inner + side
+
+            @pl.when(seq_place != target)
+            def _():
+                for slot in range(mixed_per):
+                    channel = side * mixed_per + slot
+                    full_copy(first, last, channel, slot, target, 2).start()
+
+    def send_split(first, last, chan):
+        @pl.when(on_left)
+        def _():
+            for step in range(half):
+                side = step // 2 * 2 + lax.rem(step + seq_place, 2)
+                full_copy(
+                    max(first, 1), last, split_channel(side, chan), chan, half + side, 0
+                ).start()
+            each_other(
+                side_place,
+                half,
+                lambda side: half_copy(
+                    first, last, split_channel(side, chan), chan, side
+                ).start(),
+            )
+
+        @pl.when(on_right)
+        def _():
+            each_other(
+                side_place,
+                half,
+                lambda side: full_copy(
+                    first, last, split_channel(side, chan), chan, half + side, 0
+                ).start(),
+            )
+
+    def conv_copy(channel, slot, count, target):
+        part = jnp.where(jnp.logical_and(on_right, target < half), channels, 0)
+        return remote(
+            conv_send.at[target, pl.ds(pl.multiple_of(slot * rows, 8), count * rows)],
+            conv_recv.at[pl.ds(pl.multiple_of((part + channel) * rows, 8), count * rows)],
+            send_sem.at[3],
+            back_sem.at[0],
+            {"seq": target, "ch": ch_place},
+        )
+
+    def lag_row(channel):
+        return pl.multiple_of((ch_place * channels + channel) * sub_rows, 8)
+
+    def lag_copy(channel, slot, count, target):
+        part = jnp.where(jnp.logical_and(on_right, target < left_total), all_channels, 0)
+        return remote(
+            lag_send.at[target, pl.ds(pl.multiple_of(slot * sub_rows, 8), count * sub_rows)],
+            lag_recv.at[
                 pl.ds(
-                    pl.multiple_of((seq_place * per + group * joint) * rows, 8), joint * rows
+                    pl.multiple_of(part * sub_rows + lag_row(channel), 8), count * sub_rows
                 )
             ],
-            send_sem.at[1],
-            conv_recv_sem.at[group],
-            {"seq": target, "ch": ch_place},
-        )
-
-    def lag_row(flat):
-        channel = lax.rem(flat, ch_count) * channels + (flat // ch_count) * per
-        return pl.multiple_of(channel * sub_rows, 8)
-
-    def lag_copy(target):
-        return remote(
-            lag_send.at[target],
-            lag_recv.at[pl.ds(lag_row(flat_place), per * sub_rows)],
-            send_sem.at[2],
-            lag_recv_sem.at[0],
+            send_sem.at[4],
+            back_sem.at[1],
             {"seq": target // ch_count, "ch": lax.rem(target, ch_count)},
         )
 
@@ -478,12 +586,8 @@
 
     pl.semaphore_wait(barrier, total - 1)
 
-    def send_fwd(first, last, chan):
-        each_other(
-            seq_place, seq_count, lambda target: fwd_copy(first, last, chan, target).start()
-        )
-
-    send_fwd(0, 2, 0)
+    send_mixed(0, 2)
+    send_split(0, 2, 0)
 
     first_chan = pl.multiple_of(ch_place * channels, 8)
     local_rates = rate_buf[pl.ds(first_chan, channels), :]
@@ -501,29 +605,72 @@
         lo = outer * chunk * lanes
         block = split_value(feat_ref[:, lo : lo + chunk * lanes])
         values = dot_split(local_weight, block)
-        for inner in range(chunk):
-            index = outer * chunk + inner
+        for inside in range(chunk):
+            index = outer * chunk + inside
             window = window_of(local_rates, (seq_place * rows + index) * lanes)
-            to_rows(2, index, values[:, inner * lanes : (inner + 1) * lanes] * window)
-
-    send_fwd(2, 3, 0)
+            to_rows(2, index, values[:, inside * lanes : (inside + 1) * lanes] * window)
+
+    send_mixed(2, 3)
+    send_split(2, 3, 0)
 
     def send_rest(chan, carry):
-        send_fwd(0, 3, chan)
+        send_split(0, 3, chan)
         return carry
 
-    lax.fori_loop(1, per, send_rest, 0)
-
-    own_rows = pl.ds(pl.multiple_of(seq_place * rows, 8), rows)
-
-    def keep_own(chan, carry):
-        for which in range(3):
-            gather_buf[which, chan, own_rows, :] = send_buf[
-                which, pl.ds(pl.multiple_of((seq_place * per + chan) * rows, 8), rows), :
-            ]
-        return carry
-
-    lax.fori_loop(0, per, keep_own, 0)
+    lax.fori_loop(1, jnp.where(on_right, 2, per), send_rest, 0)
+
+    conv_recv[pl.ds(channels * rows, mixed * rows), :] = jnp.zeros(
+        (mixed * rows, lanes), jnp.float32
+    )
+    for group in range(ch_count):
+        lag_recv[pl.ds((all_channels + group * channels) * sub_rows, mixed * sub_rows), :] = (
+            jnp.zeros((mixed * sub_rows, lanes), jnp.float32)
+        )
+
+    @pl.when(on_right)
+    def _():
+        conv_recv[pl.ds((channels + mixed) * rows, (channels - mixed) * rows), :] = jnp.zeros(
+            ((channels - mixed) * rows, lanes), jnp.float32
+        )
+        for group in range(ch_count):
+            lag_recv[
+                pl.ds(
+                    (all_channels + group * channels + mixed) * sub_rows,
+                    (channels - mixed) * sub_rows,
+                ),
+                :,
+            ] = jnp.zeros(((channels - mixed) * sub_rows, lanes), jnp.float32)
+
+        def keep_own(chan, carry):
+            gather_full[0, chan, pl.ds(0, half * rows), :] = jnp.zeros(
+                (half * rows, lanes), jnp.float32
+            )
+            for which in range(3):
+                gather_full[which, chan, rows_of(seq_place), :] = send_buf[
+                    which, rows_of(split_channel(side_place, chan)), :
+                ]
+            return carry
+
+        lax.fori_loop(0, per, keep_own, 0)
+
+    @pl.when(on_left)
+    def _():
+        def keep_own(chan, carry):
+            for which in range(3):
+                gather_half[which, chan, rows_of(side_place), :] = send_buf[
+                    which, rows_of(split_channel(side_place, chan)), :
+                ]
+            return carry
+
+        lax.fori_loop(0, per, keep_own, 0)
+
+    @pl.when(on_inner)
+    def _():
+        for slot in range(mixed_per):
+            for which in range(3):
+                gather_full[which, slot, rows_of(seq_place), :] = send_buf[
+                    which, rows_of((seq_place - inner) * mixed_per + slot), :
+                ]
 
     for index in range(sub_rows):
         window_buf[index] = window_of(rate_buf[...], (flat_place * sub_rows + index) * lanes)
@@ -531,102 +678,190 @@
     for load in loads[3:]:
         load.wait()
 
-    def work(chan, carry):
-        fwd_arrived(chan)
-
-        twist_cos, twist_sin = twist_ref[0], twist_ref[1]
-        packed = jnp.concatenate([gather_buf[which, chan] for which in range(3)], axis=1)
-        spread = dot_split((row_ref[0], row_ref[1]), split_value(packed))
-        turned = []
-        for which in range(3):
-            re_part = spread[:data_rows, which * lanes : (which + 1) * lanes]
-            im_part = spread[data_rows:, which * lanes : (which + 1) * lanes]
-            turned.append(
-                jnp.concatenate(
-                    [
-                        re_part * twist_cos - im_part * twist_sin,
-                        re_part * twist_sin + im_part * twist_cos,
-                    ],
-                    axis=1,
+    def send_back(channel, slot, count, seq_targets, flat_targets):
+        each_other(
+            seq_place,
+            seq_targets,
+            lambda target: conv_copy(channel, slot, count, target).start(),
+        )
+        each_other(
+            flat_place,
+            flat_targets,
+            lambda target: lag_copy(channel, slot, count, target).start(),
+        )
+
+    def work_full(chan, carry):
+        @pl.when(on_right)
+        def _():
+            @pl.when(chan + 2 < per)
+            def _():
+                each_other(
+                    side_place,
+                    half,
+                    lambda side: full_copy(
+                        0, 3, split_channel(side, chan + 2), chan + 2, half + side, 0
+                    ).start(),
                 )
-            )
-        freqs = [
-            dot_split(split_value(part), (lane_ref[0], lane_ref[1])) for part in turned
-        ]
-        grad_re, grad_im = freqs[0][:, :lanes], freqs[0][:, lanes:]
-
-        def inverse(spectrum):
-            re_part, im_part = spectrum[:, :lanes], spectrum[:, lanes:]
-            product = jnp.concatenate(
-                [
-                    re_part * grad_re + im_part * grad_im,
-                    re_part * grad_im - im_part * grad_re,
-                ],
-                axis=1,
-            )
-            back = dot_split(split_value(product), (lane_back_ref[0], lane_back_ref[1]))
-            re_part, im_part = back[:, :lanes], back[:, lanes:]
-            return jnp.concatenate(
-                [
-                    re_part * twist_cos + im_part * twist_sin,
-                    im_part * twist_cos - re_part * twist_sin,
-                ],
-                axis=0,
-            )
-
-        both = jnp.concatenate([inverse(freqs[2]), inverse(freqs[1])], axis=1)
-        final = dot_split((row_back_ref[0], row_back_ref[1]), split_value(both))
-        conv_send[:, pl.ds(pl.multiple_of(chan * rows, 8), rows), :] = final[:, :lanes].reshape(
+
+            counted((5 * half - 3) * rows, send_sem.at[0], full_sem.at[chan]).wait_recv()
+
+        @pl.when(on_left)
+        def _():
+            counted(3 * (seq_count - 1) * rows, send_sem.at[0], full_sem.at[chan]).wait_recv()
+
+        final = correlate(
+            [gather_full[which, chan] for which in range(3)],
+            row_ref,
+            row_back_ref,
+            lane_ref,
+            lane_back_ref,
+            twist_ref,
+        )
+        slot = jnp.where(on_right, chan, per + chan)
+        channel = jnp.where(
+            on_right,
+            split_channel(side_place, chan),
+            (seq_place - inner) * mixed_per + chan,
+        )
+        conv_send[:, pl.ds(pl.multiple_of(slot * rows, 8), rows), :] = final[:, :lanes].reshape(
             seq_count, rows, lanes
         )
-        lag_send[:, pl.ds(pl.multiple_of(chan * sub_rows, 8), sub_rows), :] = final[
+        lag_send[:, pl.ds(pl.multiple_of(slot * sub_rows, 8), sub_rows), :] = final[
             :, lanes:
         ].reshape(total, sub_rows, lanes)
 
-        @pl.when(lax.rem(chan, joint) == joint - 1)
+        alone = chan >= 0
+
+        @pl.when(jnp.logical_and(on_right, alone))
         def _():
-            group = chan // joint
-            each_other(seq_place, seq_count, lambda target: conv_copy(group, target).start())
+            send_back(channel, slot, 1, seq_count, total)
+
+        @pl.when(
+            jnp.logical_or(
+                jnp.logical_and(
+                    on_right, jnp.logical_and(lax.rem(chan, 2) == 0, jnp.logical_not(alone))
+                ),
+                jnp.logical_and(on_left, chan == 1),
+            )
+        )
+        def _():
+            send_back(channel - 1, slot - 1, 2, seq_count, total)
 
         return carry
 
-    lax.fori_loop(0, per, work, 0)
-    each_other(flat_place, total, lambda target: lag_copy(target).start())
-    conv_recv[pl.ds(pl.multiple_of(seq_place * per * rows, 8), per * rows), :] = conv_send[
-        seq_place
-    ]
-    lag_recv[pl.ds(lag_row(flat_place), per * sub_rows), :] = lag_send[flat_place]
-
-    here = {"seq": seq_place, "ch": ch_place}
-    for group in range(per // joint):
-        part = conv_recv.at[pl.ds(0, (seq_count - 1) * joint * rows)]
-        remote(part, part, send_sem.at[1], conv_recv_sem.at[group], here).wait_recv()
+    rounds = jnp.where(on_right, per, jnp.where(on_inner, mixed_per, 0))
+    lax.fori_loop(0, rounds, work_full, 0)
+
+    def work_half(chan, carry):
+        counted(3 * (half - 1) * rows, send_sem.at[0], half_sem.at[chan]).wait_recv()
+        final = correlate(
+            [gather_half[which, chan] for which in range(3)],
+            half_row_ref,
+            half_back_ref,
+            lane_ref,
+            lane_back_ref,
+            half_twist_ref,
+        )
+        channel = split_channel(side_place, chan)
+        conv_send[:half, pl.ds(pl.multiple_of(chan * rows, 8), rows), :] = final[
+            :, :lanes
+        ].reshape(half, rows, lanes)
+        lag_send[:left_total, pl.ds(pl.multiple_of(chan * sub_rows, 8), sub_rows), :] = final[
+            :, lanes:
+        ].reshape(left_total, sub_rows, lanes)
+
+        @pl.when(lax.rem(chan, 2) == 1)
+        def _():
+            send_back(channel - 1, chan - 1, 2, half, left_total)
+
+        @pl.when(chan == per - 1)
+        def _():
+            send_back(channel, chan, 1, half, left_total)
+
+        return carry
+
+    @pl.when(on_left)
+    def _():
+        lax.fori_loop(0, per, work_half, 0)
+
+    def keep_back(channel, slot, count):
+        conv_recv[pl.ds(pl.multiple_of(channel * rows, 8), count * rows), :] = conv_send[
+            seq_place, pl.ds(pl.multiple_of(slot * rows, 8), count * rows), :
+        ]
+        lag_recv[pl.ds(lag_row(channel), count * sub_rows), :] = lag_send[
+            flat_place, pl.ds(pl.multiple_of(slot * sub_rows, 8), count * sub_rows), :
+        ]
+
+    keep_back(split_channel(side_place, 0), 0, per)
+
+    @pl.when(on_inner)
+    def _():
+        keep_back((seq_place - inner) * mixed_per, per, mixed_per)
+
+    def expect(recv, unit, own_side, whole):
+        for place, count in (
+            (on_outer, own_side * per + whole * mixed_per + (own_side + 1) * per),
+            (on_inner, own_side * per + (whole - 1) * mixed_per + (own_side + 1) * per),
+            (on_right, own_side * per + whole * mixed_per),
+        ):
+
+            @pl.when(place)
+            def _():
+                counted(count * unit, send_sem.at[0], recv).wait_recv()
+
+    def sent(index, outer_count, inner_count, right_count):
+        for place, count in (
+            (on_outer, outer_count),
+            (on_inner, inner_count),
+            (on_right, right_count),
+        ):
+            if count:
+
+                @pl.when(place)
+                def _():
+                    counted(count, send_sem.at[index], back_sem.at[0]).wait_send()
+
+    expect(back_sem.at[0], rows, half - 1, inner)
     local_bias = bias_buf[pl.ds(first_chan, channels), :]
     for index in range(rows):
         span = slice(index * lanes, (index + 1) * lanes)
         in_grad_ref[:, span] = (
-            conv_recv[pl.ds(index, channels, stride=rows), :] + local_bias * grad_ref[:, span]
-        )
-    in_grad_store = pltpu.make_async_copy(in_grad_ref, in_grad_hbm, store_sem.at[0])
-    in_grad_store.start()
-
-    part = send_buf.at[:, pl.ds(0, (seq_count - 1) * per * rows)]
-    remote(part, part, send_sem.at[0], fwd_recv_sem.at[0], here).wait_send()
-    part = conv_recv.at[pl.ds(0, (seq_count - 1) * per * rows)]
-    remote(part, part, send_sem.at[1], conv_recv_sem.at[0], here).wait_send()
-    part = lag_send.at[pl.ds(0, total - 1)]
-    remote(part, part, send_sem.at[2], lag_recv_sem.at[0], here).wait_send()
-    remote(part, part, send_sem.at[2], lag_recv_sem.at[0], here).wait_recv()
+            conv_recv[pl.ds(index, channels, stride=rows), :]
+            + conv_recv[pl.ds(channels * rows + index, channels, stride=rows), :]
+            + local_bias * grad_ref[:, span]
+        )
+
+    to_left = 2 * half * per * rows
+    own_side = 3 * (half - 1) * per * rows
+    to_inner = 3 * mixed * rows
+    to_inner_own = 3 * (mixed - mixed_per) * rows
+    sent(0, to_left, to_left, own_side)
+    sent(1, own_side, own_side, 0)
+    sent(2, to_inner, to_inner_own, to_inner)
+    side_back = (half - 1) * per * rows
+    sent(
+        3,
+        side_back,
+        side_back + (seq_count - 1) * mixed_per * rows,
+        (seq_count - 1) * per * rows,
+    )
+    side_lag = (left_total - 1) * per * sub_rows
+    sent(
+        4,
+        side_lag,
+        side_lag + (total - 1) * mixed_per * sub_rows,
+        (total - 1) * per * sub_rows,
+    )
+    expect(back_sem.at[1], sub_rows, left_total - 1, inner * ch_count)
     weight = split_value(weight_ref[...])
     for index in range(sub_rows):
-        tile = lag_recv[pl.ds(index, all_channels, stride=sub_rows), :] * window_buf[index]
+        tile = (
+            lag_recv[pl.ds(index, all_channels, stride=sub_rows), :]
+            + lag_recv[pl.ds(all_channels * sub_rows + index, all_channels, stride=sub_rows), :]
+        ) * window_buf[index]
         feat_grad_ref[:, index * lanes : (index + 1) * lanes] = dot_split(
             weight, split_value(tile)
         )
-    feat_store = pltpu.make_async_copy(feat_grad_ref, feat_grad_hbm, store_sem.at[1])
-    feat_store.start()
-    in_grad_store.wait()
-    feat_store.wait()
 
 
 def local_whole(seq_count, ch_count, tables, *args):
@@ -634,7 +869,8 @@
     channels, local_len = out_grad.shape
     rows = local_len // lanes
     feats, all_channels = filter_weight.shape
-    per = channels // seq_count
+    half, inner, mixed, mixed_per, per = plan(seq_count, channels)
+    slots = per + mixed_per
     data_rows = rows * seq_count
     sub_rows = rows // ch_count
     total = seq_count * ch_count
@@ -643,36 +879,42 @@
     anywhere = pl.BlockSpec(memory_space=pl.ANY)
     dma = pltpu.SemaphoreType.DMA
     f32 = jnp.float32
-    return pl.pallas_call(
+    longest = max(
+        3 * channels * rows,
+        2 * channels * rows,
+        2 * all_channels * sub_rows,
+        seq_count * slots * rows,
+        total * slots * sub_rows,
+    )
+    held = pl.pallas_call(
         functools.partial(whole_kernel, sizes),
         out_shape=(
-            jax.ShapeDtypeStruct((channels, local_len), f32),
-            jax.ShapeDtypeStruct((feats, sub_rows * lanes), f32),
+            pltpu.VMEM((channels, local_len), f32),
+            pltpu.VMEM((feats, sub_rows * lanes), f32),
         ),
-        in_specs=[anywhere] * 3 + [in_vmem] * 3 + [anywhere] * 5,
-        out_specs=(anywhere, anywhere),
+        in_specs=[anywhere] * 3 + [in_vmem] * 3 + [anywhere] * len(tables),
+        out_specs=(in_vmem, in_vmem),
         scratch_shapes=[
             pltpu.VMEM((channels, local_len), f32),
             pltpu.VMEM((channels, local_len), f32),
             pltpu.VMEM((feats, local_len), f32),
             *[pltpu.VMEM(table.shape, table.dtype) for table in tables],
-            dma((8,)),
-            pltpu.VMEM((channels, local_len), f32),
-            pltpu.VMEM((feats, sub_rows * lanes), f32),
+            dma((3 + len(tables),)),
             pltpu.VMEM((3, channels * rows, lanes), f32),
             pltpu.VMEM((3, per, data_rows, lanes), f32),
-            pltpu.VMEM((seq_count, per * rows, lanes), f32),
-            pltpu.VMEM((total, per * sub_rows, lanes), f32),
-            pltpu.VMEM((channels * rows, lanes), f32),
-            pltpu.VMEM((all_channels * sub_rows, lanes), f32),
+            pltpu.VMEM((3, per, half * rows, lanes), f32),
+            pltpu.VMEM((seq_count, slots * rows, lanes), f32),
+            pltpu.VMEM((total, slots * sub_rows, lanes), f32),
+            pltpu.VMEM((2 * channels * rows, lanes), f32),
+            pltpu.VMEM((2 * all_channels * sub_rows, lanes), f32),
             pltpu.VMEM((sub_rows, all_channels, lanes), f32),
             pltpu.VMEM((all_channels, lanes), f32),
             pltpu.VMEM((all_channels, lanes), f32),
             pltpu.VMEM((all_channels, feats), f32),
+            pltpu.VMEM((longest, lanes), f32),
             dma((per,)),
-            dma((per // math.gcd(per, conv_joint),)),
-            dma((3,)),
-            dma((1,)),
+            dma((per,)),
+            dma((5,)),
             dma((2,)),
         ],
         compiler_params=pltpu.CompilerParams(collective_id=0, has_side_effects=True),
@@ -685,6 +927,25 @@
         skip_bias.reshape(1, all_channels),
         *[jnp.asarray(table) for table in tables],
     )
+    held = [pltpu.with_memory_space_constraint(value, pltpu.VMEM) for value in held]
+    return pl.pallas_call(
+        store_kernel,
+        out_shape=tuple(jax.ShapeDtypeStruct(value.shape, f32) for value in held),
+        in_specs=[in_vmem] * 2,
+        out_specs=(anywhere, anywhere),
+        scratch_shapes=[dma((2,))],
+    )(*held)
+
+
+def store_kernel(first_ref, second_ref, first_hbm, second_hbm, sem):
+    stores = [
+        pltpu.make_async_copy(first_ref, first_hbm, sem.at[0]),
+        pltpu.make_async_copy(second_ref, second_hbm, sem.at[1]),
+    ]
+    for store in stores:
+        store.start()
+    for store in stores:
+        store.wait()
 
 
 def solution(mesh):
@@ -696,16 +957,23 @@
         channels, full_len = args[0].shape
         channels = channels // ch_count
         local_len = full_len // seq_count
+        half, inner, mixed, mixed_per, per = plan(seq_count, channels)
         fits = (
-            seq_count % 2 == 0
-            and channels % seq_count == 0
+            seq_count % 4 == 0
             and channels % 8 == 0
+            and mixed == inner * mixed_per
+            and mixed_per == 2
+            and mixed + half * per == channels
+            and per % 2 == 1
+            and per >= 5
             and local_len % (8 * lanes * ch_count) == 0
             and full_len <= 512 * lanes
         )
         body = local
         if fits:
-            tables = make_tables(full_len // lanes)
+            row, row_back, lane, lane_back, twist = make_tables(full_len // lanes)
+            half_row, half_back, _, _, half_twist = make_tables(full_len // lanes // 2)
+            tables = (row, row_back, lane, lane_back, twist, half_row, half_back * 2, half_twist)
             body = functools.partial(local_whole, seq_count, ch_count, tables)
         return jax.shard_map(
             body, mesh=mesh, in_specs=in_specs, out_specs=out_specs, check_vma=False

time: 67.8 us -> 63.5 us (0.937)
  the two profiles are of different devices: /device:TPU:15 before, /device:TPU:0 now
where the time goes in v2:
time: 63.5 us; the launch traced here: 63.4 us
  Pallas kernels  62.7 us (99%)
  between operations  0.64 us (1%)
    pallas_call x1, Pallas kernels, local_whole(): pl.pallas_call(functools.partial(whole_kernel, sizes), out_shape=(pltpu.V...  61.8 us

profile of v2, /device:TPU:0, one launch (start us, length us, event | category | flops | bytes accessed | tf_op | source)
XLA Modules:
  0.0 63.4 jit_solution(12616845350557866980)
XLA Ops:
  0.6 61.8 %shard_map.149 = (f32[32,4096]{1,0:T(8,128)S(1)}, f32[64,1024]{1,0:T(8,128)S(1)}) custom-call(f32[32,4096]{1,0:T(8,128)} %refs_0_.1, f32[32,4096]{1,0:T(8,128)} %refs_1_.1, f32[64,4096]{1,0:T(8,128)} %refs_2_.1, f32[64,128]{1,0:T(8,128)} %refs_3_.1, f32[1,128]{1,0:T(1,128)} %bitcast.2, f32[1,128]{1,0:T(1,128)} %bitcast.3, ...), custom_call_target="tpu_custom_call" | custom-call | tf_op jit(solution)/shard_map/pallas_call | solution.py:889
  62.5 0.9 %shard_map.150 = (f32[32,4096]{1,0:T(8,128)}, f32[64,1024]{1,0:T(8,128)}) custom-call(f32[32,4096]{1,0:T(8,128)S(1)} %get-tuple-element.4.first_ref, f32[64,1024]{1,0:T(8,128)S(1)} %get-tuple-element.5.second_ref), custom_call_target="tpu_custom_call" | custom-call | tf_op jit(solution)/shard_map/pallas_call | solution.py:931

commit v3 on v2

--- a/solution.py
+++ b/solution.py
@@ -316,13 +316,14 @@
     return product(left[0], right[0]) + (product(left[0], right[1]) + product(left[1], right[0]))
 
 
-def correlate(pieces, row_ref, row_back_ref, lane_ref, lane_back_ref, twist_ref):
+def spectra(pieces, tables):
+    row_ref, lane_ref, twist_ref = tables[0], tables[2], tables[4]
     data_rows = pieces[0].shape[0]
     twist_cos, twist_sin = twist_ref[0], twist_ref[1]
-    packed = jnp.concatenate(pieces, axis=1)
+    packed = pieces[0] if len(pieces) == 1 else jnp.concatenate(pieces, axis=1)
     spread = dot_split((row_ref[0], row_ref[1]), split_value(packed))
     freqs = []
-    for which in range(3):
+    for which in range(len(pieces)):
         re_part = spread[:data_rows, which * lanes : (which + 1) * lanes]
         im_part = spread[data_rows:, which * lanes : (which + 1) * lanes]
         turned = jnp.concatenate(
@@ -333,9 +334,15 @@
             axis=1,
         )
         freqs.append(dot_split(split_value(turned), (lane_ref[0], lane_ref[1])))
-    grad_re, grad_im = freqs[0][:, :lanes], freqs[0][:, lanes:]
-
-    def inverse(spectrum):
+    return freqs
+
+
+def correlated(grad_freqs, others, tables):
+    row_back_ref, lane_back_ref, twist_ref = tables[1], tables[3], tables[4]
+    twist_cos, twist_sin = twist_ref[0], twist_ref[1]
+    grad_re, grad_im = grad_freqs[:, :lanes], grad_freqs[:, lanes:]
+    turned = []
+    for spectrum in others:
         re_part, im_part = spectrum[:, :lanes], spectrum[:, lanes:]
         product = jnp.concatenate(
             [
@@ -346,15 +353,16 @@
         )
         back = dot_split(split_value(product), (lane_back_ref[0], lane_back_ref[1]))
         re_part, im_part = back[:, :lanes], back[:, lanes:]
-        return jnp.concatenate(
-            [
-                re_part * twist_cos + im_part * twist_sin,
-                im_part * twist_cos - re_part * twist_sin,
-            ],
-            axis=0,
-        )
-
-    both = jnp.concatenate([inverse(freqs[2]), inverse(freqs[1])], axis=1)
+        turned.append(
+            jnp.concatenate(
+                [
+                    re_part * twist_cos + im_part * twist_sin,
+                    im_part * twist_cos - re_part * twist_sin,
+                ],
+                axis=0,
+            )
+        )
+    both = turned[0] if len(turned) == 1 else jnp.concatenate(turned, axis=1)
     return dot_split((row_back_ref[0], row_back_ref[1]), split_value(both))
 
 
@@ -407,10 +415,13 @@
         bias_buf,
         weight_buf,
         ruler,
+        grad_freqs,
         full_sem,
+        filt_sem,
         half_sem,
         send_sem,
         back_sem,
+        met_sem,
     ) = refs
     seq_count, ch_count, channels, rows = sizes
     half, inner, mixed, mixed_per, per = plan(seq_count, channels)
@@ -450,17 +461,15 @@
     ]
     barrier = pltpu.get_barrier_semaphore()
 
-    def greet(step, carry):
-        other = lax.rem(flat_place + step, total)
+    def signal(sem, seq, ch):
         pl.semaphore_signal(
-            barrier,
-            inc=1,
-            device_id={"seq": other // ch_count, "ch": lax.rem(other, ch_count)},
-            device_id_type=pl.DeviceIdType.MESH,
-        )
-        return carry
-
-    lax.fori_loop(1, total, greet, 0)
+            sem, inc=1, device_id={"seq": seq, "ch": ch}, device_id_type=pl.DeviceIdType.MESH
+        )
+
+    for step in range(1, seq_count):
+        signal(barrier, lax.rem(seq_place + step, seq_count), ch_place)
+    for step in range(1, ch_count):
+        signal(barrier, seq_place, lax.rem(ch_place + step, ch_count))
     for load in loads:
         load.start()
 
@@ -496,7 +505,7 @@
             send_buf.at[first:last, rows_of(channel)],
             gather_full.at[first:last, slot, rows_of(seq_place)],
             send_sem.at[sem],
-            full_sem.at[slot],
+            (filt_sem if first == 2 else full_sem).at[slot],
             {"seq": target, "ch": ch_place},
         )
 
@@ -519,7 +528,7 @@
                     channel = side * mixed_per + slot
                     full_copy(first, last, channel, slot, target, 2).start()
 
-    def send_split(first, last, chan):
+    def to_right(first, last, chan):
         @pl.when(on_left)
         def _():
             for step in range(half):
@@ -527,13 +536,6 @@
                 full_copy(
                     max(first, 1), last, split_channel(side, chan), chan, half + side, 0
                 ).start()
-            each_other(
-                side_place,
-                half,
-                lambda side: half_copy(
-                    first, last, split_channel(side, chan), chan, side
-                ).start(),
-            )
 
         @pl.when(on_right)
         def _():
@@ -542,6 +544,17 @@
                 half,
                 lambda side: full_copy(
                     first, last, split_channel(side, chan), chan, half + side, 0
+                ).start(),
+            )
+
+    def to_left(first, last, chan):
+        @pl.when(on_left)
+        def _():
+            each_other(
+                side_place,
+                half,
+                lambda side: half_copy(
+                    first, last, split_channel(side, chan), chan, side
                 ).start(),
             )
 
@@ -584,10 +597,14 @@
     for index in range(rows):
         to_rows(1, index, input_ref[:, index * lanes : (index + 1) * lanes])
 
-    pl.semaphore_wait(barrier, total - 1)
+    pl.semaphore_wait(barrier, seq_count + ch_count - 2)
 
     send_mixed(0, 2)
-    send_split(0, 2, 0)
+    to_right(0, 2, 0)
+    to_left(0, 2, 0)
+
+    for step in range(1, seq_count):
+        signal(met_sem.at[0], lax.rem(seq_place + step, seq_count), ch_place)
 
     first_chan = pl.multiple_of(ch_place * channels, 8)
     local_rates = rate_buf[pl.ds(first_chan, channels), :]
@@ -611,10 +628,13 @@
             to_rows(2, index, values[:, inside * lanes : (inside + 1) * lanes] * window)
 
     send_mixed(2, 3)
-    send_split(2, 3, 0)
+    to_right(2, 3, 0)
+    to_left(2, 3, 0)
 
     def send_rest(chan, carry):
-        send_split(0, 3, chan)
+        to_right(0, 2, chan)
+        to_right(2, 3, chan)
+        to_left(0, 3, chan)
         return carry
 
     lax.fori_loop(1, jnp.where(on_right, 2, per), send_rest, 0)
@@ -677,76 +697,66 @@
 
     for load in loads[3:]:
         load.wait()
-
-    def send_back(channel, slot, count, seq_targets, flat_targets):
+    pl.semaphore_wait(met_sem.at[0], seq_count - 1)
+
+    def send_conv(channel, slot, count, targets):
         each_other(
             seq_place,
-            seq_targets,
+            targets,
             lambda target: conv_copy(channel, slot, count, target).start(),
         )
+
+    def send_lag(channel, slot, count, targets):
         each_other(
             flat_place,
-            flat_targets,
+            targets,
             lambda target: lag_copy(channel, slot, count, target).start(),
         )
 
+    full_tables = (row_ref, row_back_ref, lane_ref, lane_back_ref, twist_ref)
+    half_tables = (half_row_ref, half_back_ref, lane_ref, lane_back_ref, half_twist_ref)
+
     def work_full(chan, carry):
-        @pl.when(on_right)
-        def _():
-            @pl.when(chan + 2 < per)
-            def _():
-                each_other(
-                    side_place,
-                    half,
-                    lambda side: full_copy(
-                        0, 3, split_channel(side, chan + 2), chan + 2, half + side, 0
-                    ).start(),
-                )
-
-            counted((5 * half - 3) * rows, send_sem.at[0], full_sem.at[chan]).wait_recv()
-
-        @pl.when(on_left)
-        def _():
-            counted(3 * (seq_count - 1) * rows, send_sem.at[0], full_sem.at[chan]).wait_recv()
-
-        final = correlate(
-            [gather_full[which, chan] for which in range(3)],
-            row_ref,
-            row_back_ref,
-            lane_ref,
-            lane_back_ref,
-            twist_ref,
-        )
         slot = jnp.where(on_right, chan, per + chan)
         channel = jnp.where(
             on_right,
             split_channel(side_place, chan),
             (seq_place - inner) * mixed_per + chan,
         )
-        conv_send[:, pl.ds(pl.multiple_of(slot * rows, 8), rows), :] = final[:, :lanes].reshape(
-            seq_count, rows, lanes
-        )
-        lag_send[:, pl.ds(pl.multiple_of(slot * sub_rows, 8), sub_rows), :] = final[
-            :, lanes:
-        ].reshape(total, sub_rows, lanes)
-
-        alone = chan >= 0
-
-        @pl.when(jnp.logical_and(on_right, alone))
+
+        @pl.when(on_right)
         def _():
-            send_back(channel, slot, 1, seq_count, total)
-
-        @pl.when(
-            jnp.logical_or(
-                jnp.logical_and(
-                    on_right, jnp.logical_and(lax.rem(chan, 2) == 0, jnp.logical_not(alone))
-                ),
-                jnp.logical_and(on_left, chan == 1),
-            )
-        )
+            @pl.when(chan + 2 < per)
+            def _():
+                to_right(0, 2, chan + 2)
+                to_right(2, 3, chan + 2)
+
+            counted((3 * half - 2) * rows, send_sem.at[0], full_sem.at[chan]).wait_recv()
+
+        @pl.when(on_left)
         def _():
-            send_back(channel - 1, slot - 1, 2, seq_count, total)
-
+            counted(2 * (seq_count - 1) * rows, send_sem.at[0], full_sem.at[chan]).wait_recv()
+
+        first, second = spectra([gather_full[0, chan], gather_full[1, chan]], full_tables)
+        grad_freqs[...] = first
+        lag_send[:, pl.ds(pl.multiple_of(slot * sub_rows, 8), sub_rows), :] = correlated(
+            first, [second], full_tables
+        ).reshape(total, sub_rows, lanes)
+        send_lag(channel, slot, 1, total)
+
+        @pl.when(on_right)
+        def _():
+            counted((2 * half - 1) * rows, send_sem.at[0], filt_sem.at[chan]).wait_recv()
+
+        @pl.when(on_left)
+        def _():
+            counted((seq_count - 1) * rows, send_sem.at[0], filt_sem.at[chan]).wait_recv()
+
+        (third,) = spectra([gather_full[2, chan]], full_tables)
+        conv_send[:, pl.ds(pl.multiple_of(slot * rows, 8), rows), :] = correlated(
+            grad_freqs[...], [third], full_tables
+        ).reshape(seq_count, rows, lanes)
+        send_conv(channel, slot, 1, seq_count)
         return carry
 
     rounds = jnp.where(on_right, per, jnp.where(on_inner, mixed_per, 0))
@@ -754,14 +764,10 @@
 
     def work_half(chan, carry):
         counted(3 * (half - 1) * rows, send_sem.at[0], half_sem.at[chan]).wait_recv()
-        final = correlate(
-            [gather_half[which, chan] for which in range(3)],
-            half_row_ref,
-            half_back_ref,
-            lane_ref,
-            lane_back_ref,
-            half_twist_ref,
-        )
+        first, second, third = spectra(
+            [gather_half[which, chan] for which in range(3)], half_tables
+        )
+        final = correlated(first, [third, second], half_tables)
         channel = split_channel(side_place, chan)
         conv_send[:half, pl.ds(pl.multiple_of(chan * rows, 8), rows), :] = final[
             :, :lanes
@@ -772,11 +778,13 @@
 
         @pl.when(lax.rem(chan, 2) == 1)
         def _():
-            send_back(channel - 1, chan - 1, 2, half, left_total)
+            send_conv(channel - 1, chan - 1, 2, half)
+            send_lag(channel - 1, chan - 1, 2, left_total)
 
         @pl.when(chan == per - 1)
         def _():
-            send_back(channel, chan, 1, half, left_total)
+            send_conv(channel, chan, 1, half)
+            send_lag(channel, chan, 1, left_total)
 
         return carry
 
@@ -821,37 +829,6 @@
                 def _():
                     counted(count, send_sem.at[index], back_sem.at[0]).wait_send()
 
-    expect(back_sem.at[0], rows, half - 1, inner)
-    local_bias = bias_buf[pl.ds(first_chan, channels), :]
-    for index in range(rows):
-        span = slice(index * lanes, (index + 1) * lanes)
-        in_grad_ref[:, span] = (
-            conv_recv[pl.ds(index, channels, stride=rows), :]
-            + conv_recv[pl.ds(channels * rows + index, channels, stride=rows), :]
-            + local_bias * grad_ref[:, span]
-        )
-
-    to_left = 2 * half * per * rows
-    own_side = 3 * (half - 1) * per * rows
-    to_inner = 3 * mixed * rows
-    to_inner_own = 3 * (mixed - mixed_per) * rows
-    sent(0, to_left, to_left, own_side)
-    sent(1, own_side, own_side, 0)
-    sent(2, to_inner, to_inner_own, to_inner)
-    side_back = (half - 1) * per * rows
-    sent(
-        3,
-        side_back,
-        side_back + (seq_count - 1) * mixed_per * rows,
-        (seq_count - 1) * per * rows,
-    )
-    side_lag = (left_total - 1) * per * sub_rows
-    sent(
-        4,
-        side_lag,
-        side_lag + (total - 1) * mixed_per * sub_rows,
-        (total - 1) * per * sub_rows,
-    )
     expect(back_sem.at[1], sub_rows, left_total - 1, inner * ch_count)
     weight = split_value(weight_ref[...])
     for index in range(sub_rows):
@@ -862,6 +839,37 @@
         feat_grad_ref[:, index * lanes : (index + 1) * lanes] = dot_split(
             weight, split_value(tile)
         )
+    expect(back_sem.at[0], rows, half - 1, inner)
+    local_bias = bias_buf[pl.ds(first_chan, channels), :]
+    for index in range(rows):
+        span = slice(index * lanes, (index + 1) * lanes)
+        in_grad_ref[:, span] = (
+            conv_recv[pl.ds(index, channels, stride=rows), :]
+            + conv_recv[pl.ds(channels * rows + index, channels, stride=rows), :]
+            + local_bias * grad_ref[:, span]
+        )
+
+    left_sent = 2 * half * per * rows
+    own_side = 3 * (half - 1) * per * rows
+    to_inner = 3 * mixed * rows
+    to_inner_own = 3 * (mixed - mixed_per) * rows
+    sent(0, left_sent, left_sent, own_side)
+    sent(1, own_side, own_side, 0)
+    sent(2, to_inner, to_inner_own, to_inner)
+    side_back = (half - 1) * per * rows
+    sent(
+        3,
+        side_back,
+        side_back + (seq_count - 1) * mixed_per * rows,
+        (seq_count - 1) * per * rows,
+    )
+    side_lag = (left_total - 1) * per * sub_rows
+    sent(
+        4,
+        side_lag,
+        side_lag + (total - 1) * mixed_per * sub_rows,
+        (total - 1) * per * sub_rows,
+    )
 
 
 def local_whole(seq_count, ch_count, tables, *args):
@@ -912,10 +920,13 @@
             pltpu.VMEM((all_channels, lanes), f32),
             pltpu.VMEM((all_channels, feats), f32),
             pltpu.VMEM((longest, lanes), f32),
+            pltpu.VMEM((data_rows, 2 * lanes), f32),
+            dma((per,)),
             dma((per,)),
             dma((per,)),
             dma((5,)),
             dma((2,)),
+            pltpu.SemaphoreType.REGULAR((1,)),
         ],
         compiler_params=pltpu.CompilerParams(collective_id=0, has_side_effects=True),
     )(

time: 63.5 us -> 60.6 us (0.954)
  Pallas kernels: 62.7 us -> 59.8 us
    pallas_call x1, Pallas kernels: 61.8 us -> 58.9 us  [local_whole(): pl.pallas_call(functools.partial(whole_kernel, sizes), out_shape=(pltpu.V...]
where the time goes in v3:
time: 60.6 us; the launch traced here: 60.4 us
  Pallas kernels  59.8 us (99%)
  between operations  0.64 us (1%)
    pallas_call x1, Pallas kernels, local_whole(): pl.pallas_call(functools.partial(whole_kernel, sizes), out_shape=(pltpu.V...  58.9 us

profile of v3, /device:TPU:0, one launch (start us, length us, event | category | flops | bytes accessed | tf_op | source)
XLA Modules:
  0.0 60.4 jit_solution(4807947410722881876)
XLA Ops:
  0.6 58.9 %shard_map.149 = (f32[32,4096]{1,0:T(8,128)S(1)}, f32[64,1024]{1,0:T(8,128)S(1)}) custom-call(f32[32,4096]{1,0:T(8,128)} %refs_0_.1, f32[32,4096]{1,0:T(8,128)} %refs_1_.1, f32[64,4096]{1,0:T(8,128)} %refs_2_.1, f32[64,128]{1,0:T(8,128)} %refs_3_.1, f32[1,128]{1,0:T(1,128)} %bitcast.2, f32[1,128]{1,0:T(1,128)} %bitcast.3, ...), custom_call_target="tpu_custom_call" | custom-call | tf_op jit(solution)/shard_map/pallas_call | solution.py:897
  59.5 0.9 %shard_map.150 = (f32[32,4096]{1,0:T(8,128)}, f32[64,1024]{1,0:T(8,128)}) custom-call(f32[32,4096]{1,0:T(8,128)S(1)} %get-tuple-element.4.first_ref, f32[64,1024]{1,0:T(8,128)S(1)} %get-tuple-element.5.second_ref), custom_call_target="tpu_custom_call" | custom-call | tf_op jit(solution)/shard_map/pallas_call | solution.py:942

commit v4 on v3

--- a/solution.py
+++ b/solution.py
@@ -378,9 +378,9 @@
         grad_hbm,
         input_hbm,
         feat_hbm,
-        weight_ref,
-        rate_ref,
-        bias_ref,
+        weight_hbm,
+        rate_hbm,
+        bias_hbm,
         row_hbm,
         row_back_hbm,
         lane_hbm,
@@ -402,6 +402,9 @@
         half_row_ref,
         half_back_ref,
         half_twist_ref,
+        weight_ref,
+        rate_ref,
+        bias_ref,
         load_sem,
         send_buf,
         gather_full,
@@ -447,6 +450,9 @@
             (
                 (grad_hbm, grad_ref),
                 (input_hbm, input_ref),
+                (weight_hbm, weight_ref),
+                (rate_hbm, rate_ref),
+                (bias_hbm, bias_ref),
                 (feat_hbm, feat_ref),
                 (row_hbm, row_ref),
                 (twist_hbm, twist_ref),
@@ -588,8 +594,6 @@
     def to_rows(which, index, tile):
         send_buf[which, pl.ds(index, channels, stride=rows), :] = tile
 
-    rate_buf[...] = jnp.broadcast_to(rate_ref[...], (lanes, all_channels)).T
-    weight_buf[...] = weight_ref[...].T
     loads[0].wait()
     for index in range(rows):
         to_rows(0, index, grad_ref[:, index * lanes : (index + 1) * lanes])
@@ -597,11 +601,25 @@
     for index in range(rows):
         to_rows(1, index, input_ref[:, index * lanes : (index + 1) * lanes])
 
+    for load in loads[2:5]:
+        load.wait()
+    rate_buf[...] = jnp.broadcast_to(rate_ref[...], (lanes, all_channels)).T
+    weight_buf[...] = weight_ref[...].T
+    bias_buf[...] = jnp.broadcast_to(bias_ref[...], (lanes, all_channels)).T
+
     pl.semaphore_wait(barrier, seq_count + ch_count - 2)
 
-    send_mixed(0, 2)
+    @pl.when(on_right)
+    def _():
+        send_mixed(0, 2)
+
     to_right(0, 2, 0)
     to_left(0, 2, 0)
+
+    @pl.when(on_left)
+    def _():
+        send_mixed(0, 2)
+
 
     for step in range(1, seq_count):
         signal(met_sem.at[0], lax.rem(seq_place + step, seq_count), ch_place)
@@ -615,8 +633,7 @@
         steps_t = (first + lane_ids).astype(jnp.float32) / full_len
         return jnp.exp(-rates * steps_t) + shift_term
 
-    bias_buf[...] = jnp.broadcast_to(bias_ref[...], (lanes, all_channels)).T
-    loads[2].wait()
+    loads[5].wait()
     chunk = math.gcd(rows, 4)
     for outer in range(rows // chunk):
         lo = outer * chunk * lanes
@@ -633,8 +650,8 @@
 
     def send_rest(chan, carry):
         to_right(0, 2, chan)
+        to_left(0, 3, chan)
         to_right(2, 3, chan)
-        to_left(0, 3, chan)
         return carry
 
     lax.fori_loop(1, jnp.where(on_right, 2, per), send_rest, 0)
@@ -695,7 +712,7 @@
     for index in range(sub_rows):
         window_buf[index] = window_of(rate_buf[...], (flat_place * sub_rows + index) * lanes)
 
-    for load in loads[3:]:
+    for load in loads[6:]:
         load.wait()
     pl.semaphore_wait(met_sem.at[0], seq_count - 1)
 
@@ -742,7 +759,14 @@
         lag_send[:, pl.ds(pl.multiple_of(slot * sub_rows, 8), sub_rows), :] = correlated(
             first, [second], full_tables
         ).reshape(total, sub_rows, lanes)
-        send_lag(channel, slot, 1, total)
+
+        @pl.when(on_right)
+        def _():
+            send_lag(channel, slot, 1, total)
+
+        @pl.when(jnp.logical_and(on_left, chan == 1))
+        def _():
+            send_lag(channel - 1, slot - 1, 2, total)
 
         @pl.when(on_right)
         def _():
@@ -900,14 +924,17 @@
             pltpu.VMEM((channels, local_len), f32),
             pltpu.VMEM((feats, sub_rows * lanes), f32),
         ),
-        in_specs=[anywhere] * 3 + [in_vmem] * 3 + [anywhere] * len(tables),
+        in_specs=[anywhere] * (6 + len(tables)),
         out_specs=(in_vmem, in_vmem),
         scratch_shapes=[
             pltpu.VMEM((channels, local_len), f32),
             pltpu.VMEM((channels, local_len), f32),
             pltpu.VMEM((feats, local_len), f32),
             *[pltpu.VMEM(table.shape, table.dtype) for table in tables],
-            dma((3 + len(tables),)),
+            pltpu.VMEM((feats, all_channels), f32),
+            pltpu.VMEM((1, all_channels), f32),
+            pltpu.VMEM((1, all_channels), f32),
+            dma((6 + len(tables),)),
             pltpu.VMEM((3, channels * rows, lanes), f32),
             pltpu.VMEM((3, per, data_rows, lanes), f32),
             pltpu.VMEM((3, per, half * rows, lanes), f32),

time: 60.6 us -> 59.9 us (0.988)
  Pallas kernels: 59.8 us -> 59.1 us
    pallas_call x1, Pallas kernels: 58.9 us -> 58.2 us  [local_whole(): pl.pallas_call(functools.partial(whole_kernel, sizes), out_shape=(pltpu.V...]
where the time goes in v4:
time: 59.9 us; the launch traced here: 59.7 us
  Pallas kernels  59.1 us (99%)
  between operations  0.64 us (1%)
    pallas_call x1, Pallas kernels, local_whole(): pl.pallas_call(functools.partial(whole_kernel, sizes), out_shape=(pltpu.V...  58.2 us

profile of v4, /device:TPU:0, one launch (start us, length us, event | category | flops | bytes accessed | tf_op | source)
XLA Modules:
  0.0 59.7 jit_solution(1753279096351612453)
XLA Ops:
  0.6 58.2 %shard_map.149 = (f32[32,4096]{1,0:T(8,128)S(1)}, f32[64,1024]{1,0:T(8,128)S(1)}) custom-call(f32[32,4096]{1,0:T(8,128)} %refs_0_.1, f32[32,4096]{1,0:T(8,128)} %refs_1_.1, f32[64,4096]{1,0:T(8,128)} %refs_2_.1, f32[64,128]{1,0:T(8,128)} %refs_3_.1, f32[1,128]{1,0:T(1,128)} %bitcast.2, f32[1,128]{1,0:T(1,128)} %bitcast.3, ...), custom_call_target="tpu_custom_call" | custom-call | tf_op jit(solution)/shard_map/pallas_call | solution.py:921
  58.8 0.9 %shard_map.150 = (f32[32,4096]{1,0:T(8,128)}, f32[64,1024]{1,0:T(8,128)}) custom-call(f32[32,4096]{1,0:T(8,128)S(1)} %get-tuple-element.4.first_ref, f32[64,1024]{1,0:T(8,128)S(1)} %get-tuple-element.5.second_ref), custom_call_target="tpu_custom_call" | custom-call | tf_op jit(solution)/shard_map/pallas_call | solution.py:969

commit v5 on v4

--- a/solution.py
+++ b/solution.py
@@ -746,7 +746,6 @@
             @pl.when(chan + 2 < per)
             def _():
                 to_right(0, 2, chan + 2)
-                to_right(2, 3, chan + 2)
 
             counted((3 * half - 2) * rows, send_sem.at[0], full_sem.at[chan]).wait_recv()
 
@@ -763,6 +762,10 @@
         @pl.when(on_right)
         def _():
             send_lag(channel, slot, 1, total)
+
+        @pl.when(jnp.logical_and(on_right, chan + 2 < per))
+        def _():
+            to_right(2, 3, chan + 2)
 
         @pl.when(jnp.logical_and(on_left, chan == 1))
         def _():

time: 59.9 us -> 59.5 us (level)
  no operation moved by 1% of the time
where the time goes in v5:
time: 59.5 us; the launch traced here: 59.3 us
  Pallas kernels  58.7 us (99%)
  between operations  0.64 us (1%)
    pallas_call x1, Pallas kernels, local_whole(): pl.pallas_call(functools.partial(whole_kernel, sizes), out_shape=(pltpu.V...  57.8 us

profile of v5, /device:TPU:0, one launch (start us, length us, event | category | flops | bytes accessed | tf_op | source)
XLA Modules:
  0.0 59.3 jit_solution(1197284146027085761)
XLA Ops:
  0.6 57.8 %shard_map.149 = (f32[32,4096]{1,0:T(8,128)S(1)}, f32[64,1024]{1,0:T(8,128)S(1)}) custom-call(f32[32,4096]{1,0:T(8,128)} %refs_0_.1, f32[32,4096]{1,0:T(8,128)} %refs_1_.1, f32[64,4096]{1,0:T(8,128)} %refs_2_.1, f32[64,128]{1,0:T(8,128)} %refs_3_.1, f32[1,128]{1,0:T(1,128)} %bitcast.2, f32[1,128]{1,0:T(1,128)} %bitcast.3, ...), custom_call_target="tpu_custom_call" | custom-call | tf_op jit(solution)/shard_map/pallas_call | solution.py:924
  58.4 0.9 %shard_map.150 = (f32[32,4096]{1,0:T(8,128)}, f32[64,1024]{1,0:T(8,128)}) custom-call(f32[32,4096]{1,0:T(8,128)S(1)} %get-tuple-element.4.first_ref, f32[64,1024]{1,0:T(8,128)S(1)} %get-tuple-element.5.second_ref), custom_call_target="tpu_custom_call" | custom-call | tf_op jit(solution)/shard_map/pallas_call | solution.py:972

commit v6 on v5

--- a/solution.py
+++ b/solution.py
@@ -570,7 +570,7 @@
             conv_send.at[target, pl.ds(pl.multiple_of(slot * rows, 8), count * rows)],
             conv_recv.at[pl.ds(pl.multiple_of((part + channel) * rows, 8), count * rows)],
             send_sem.at[3],
-            back_sem.at[0],
+            back_sem.at[jnp.where(part > 0, 2, 0)],
             {"seq": target, "ch": ch_place},
         )
 
@@ -833,10 +833,10 @@
     def _():
         keep_back((seq_place - inner) * mixed_per, per, mixed_per)
 
-    def expect(recv, unit, own_side, whole):
+    def expect(recv, unit, own_side, whole, across):
         for place, count in (
-            (on_outer, own_side * per + whole * mixed_per + (own_side + 1) * per),
-            (on_inner, own_side * per + (whole - 1) * mixed_per + (own_side + 1) * per),
+            (on_outer, own_side * per + whole * mixed_per + across * per),
+            (on_inner, own_side * per + (whole - 1) * mixed_per + across * per),
             (on_right, own_side * per + whole * mixed_per),
         ):
 
@@ -856,7 +856,7 @@
                 def _():
                     counted(count, send_sem.at[index], back_sem.at[0]).wait_send()
 
-    expect(back_sem.at[1], sub_rows, left_total - 1, inner * ch_count)
+    expect(back_sem.at[1], sub_rows, left_total - 1, inner * ch_count, left_total)
     weight = split_value(weight_ref[...])
     for index in range(sub_rows):
         tile = (
@@ -866,15 +866,23 @@
         feat_grad_ref[:, index * lanes : (index + 1) * lanes] = dot_split(
             weight, split_value(tile)
         )
-    expect(back_sem.at[0], rows, half - 1, inner)
+    expect(back_sem.at[0], rows, half - 1, inner, 0)
     local_bias = bias_buf[pl.ds(first_chan, channels), :]
     for index in range(rows):
         span = slice(index * lanes, (index + 1) * lanes)
         in_grad_ref[:, span] = (
-            conv_recv[pl.ds(index, channels, stride=rows), :]
-            + conv_recv[pl.ds(channels * rows + index, channels, stride=rows), :]
-            + local_bias * grad_ref[:, span]
-        )
+            conv_recv[pl.ds(index, channels, stride=rows), :] + local_bias * grad_ref[:, span]
+        )
+
+    @pl.when(on_left)
+    def _():
+        counted(half * per * rows, send_sem.at[0], back_sem.at[2]).wait_recv()
+        for index in range(rows):
+            span = slice(index * lanes, (index + 1) * lanes)
+            in_grad_ref[:, span] = (
+                in_grad_ref[:, span]
+                + conv_recv[pl.ds(channels * rows + index, channels, stride=rows), :]
+            )
 
     left_sent = 2 * half * per * rows
     own_side = 3 * (half - 1) * per * rows
@@ -955,7 +963,7 @@
             dma((per,)),
             dma((per,)),
             dma((5,)),
-            dma((2,)),
+            dma((3,)),
             pltpu.SemaphoreType.REGULAR((1,)),
         ],
         compiler_params=pltpu.CompilerParams(collective_id=0, has_side_effects=True),

time: 59.5 us -> 59.3 us (level)
  no operation moved by 1% of the time
where the time goes in v6:
time: 59.3 us; the launch traced here: 59.2 us
  Pallas kernels  58.5 us (99%)
  between operations  0.64 us (1%)
    pallas_call x1, Pallas kernels, local_whole(): pl.pallas_call(functools.partial(whole_kernel, sizes), out_shape=(pltpu.V...  57.6 us

profile of v6, /device:TPU:0, one launch (start us, length us, event | category | flops | bytes accessed | tf_op | source)
XLA Modules:
  0.0 59.2 jit_solution(10146997079975831397)
XLA Ops:
  0.6 57.6 %shard_map.149 = (f32[32,4096]{1,0:T(8,128)S(1)}, f32[64,1024]{1,0:T(8,128)S(1)}) custom-call(f32[32,4096]{1,0:T(8,128)} %refs_0_.1, f32[32,4096]{1,0:T(8,128)} %refs_1_.1, f32[64,4096]{1,0:T(8,128)} %refs_2_.1, f32[64,128]{1,0:T(8,128)} %refs_3_.1, f32[1,128]{1,0:T(1,128)} %bitcast.2, f32[1,128]{1,0:T(1,128)} %bitcast.3, ...), custom_call_target="tpu_custom_call" | custom-call | tf_op jit(solution)/shard_map/pallas_call | solution.py:932
  58.3 0.9 %shard_map.150 = (f32[32,4096]{1,0:T(8,128)}, f32[64,1024]{1,0:T(8,128)}) custom-call(f32[32,4096]{1,0:T(8,128)S(1)} %get-tuple-element.4.first_ref, f32[64,1024]{1,0:T(8,128)S(1)} %get-tuple-element.5.second_ref), custom_call_target="tpu_custom_call" | custom-call | tf_op jit(solution)/shard_map/pallas_call | solution.py:980
